TPU v7x, 128 devices: a whole 4x4x4 slice. The times are simulated.
128 devices in a mesh: row: 8 (over x, core), col: 16 (over z, y).
Axes of the slice: x: 4, y: 4, z: 4, core: 2. Of those that a mesh axis runs over, the one named last changes fastest.
Arguments:
- mask: bfloat16 [256, 4096], P('row', 'col'), may hold values from 0 to 1
- target: int32 [256, 4096], P('row', 'col'), may hold values 0 or 1
- kernels: bfloat16 [8, 2, 33, 33], replicated, may hold values from -0.1875 to 0.1875
- weights: float32 [8], replicated, may hold values from 0.2 to 1
- doses: float32 [8], replicated, may hold values from 0.8 to 1.2
- site_pix: int32 [1024, 768], P('row', 'col'), may hold values from 0 to 8191
- send_count: int32 [8, 2048], P('row', 'col'), may hold values from 0 to 48, as said below
- recv_frag: int32 [1024, 768], P('row', 'col'), may hold values from 0 to 2047
- frag_target: float32 [8, 262144], P(None, ('row', 'col')), may hold values from 0 to 6
Outputs:
- gradient: float32 [256, 4096], P('row', 'col')
- frag_error: float32 [8, 262144], P(None, ('row', 'col'))
Inputs may be any that keep to these rules, and one draw needn't show every extreme that they name: `send_count`: no device sends more than 48 live slots to one owner; in every draw one owner receives 48 live slots from every device.
All inputs are finite; a program needn't handle non-finite values. No bound on the sum of `target` on one device may be relied on, other than what follows from the above.
Results may differ from a plain program's by a relative error of at most 0.0045.
Values may be sent and summed in bfloat16 or wider, within the bound.
No kernel may reach another device: no remote copies, remote signals or barrier semaphores. Data moves between devices by JAX's collectives and lax.ppermute only.
A program may use at most 64 MiB of HBM per device.

v0:
```python
import jax
import jax.numpy as jnp
from jax import lax
from jax.sharding import PartitionSpec as P

steepness = 4.0
threshold = 1.2


def extended(block, sides, width):
    for axis, dim in sides:
        count = lax.axis_size(axis)
        forward = [(i, i + 1) for i in range(count - 1)]
        backward = [(target, source) for source, target in forward]
        low = lax.ppermute(
            lax.slice_in_dim(block, block.shape[dim] - width, None, axis=dim), axis, forward
        )
        high = lax.ppermute(lax.slice_in_dim(block, 0, width, axis=dim), axis, backward)
        block = jnp.concatenate([low, block, high], axis=dim)
    return block


def banded_table(taps, block):
    extent = taps.shape[-1]
    span = block + extent - 1
    offsets = jnp.arange(span)[:, None] - jnp.arange(block)[None, :]
    inside = (offsets >= 0) & (offsets < extent)
    picked = taps[:, :, jnp.clip(offsets, 0, extent - 1)]
    picked = jnp.where(inside[None, None], picked, jnp.zeros((), taps.dtype))
    return picked.transpose(1, 2, 0, 3).reshape(extent * span, taps.shape[0] * block)


def patches_of(padded, extent, block, out_rows, out_cols):
    span = block + extent - 1
    blocks = -(-out_cols // block)
    windows = jnp.stack(
        [padded[:, start * block : start * block + span] for start in range(blocks)], axis=1
    )
    stacked = jnp.stack([windows[offset : offset + out_rows] for offset in range(extent)], axis=2)
    return stacked.reshape(out_rows, blocks, extent * span)


def correlate_bank(padded, taps):
    extent = taps.shape[-1]
    out_rows = padded.shape[0] - extent + 1
    out_cols = padded.shape[1] - extent + 1
    block = min(out_cols, 32)
    table = banded_table(taps, block)
    patches = patches_of(padded, extent, block, out_rows, out_cols)
    product = jnp.einsum("rnk,kc->rnc", patches, table, preferred_element_type=jnp.float32)
    blocks = product.shape[1]
    product = product.reshape(out_rows, blocks, taps.shape[0], block).transpose(2, 0, 1, 3)
    return product.reshape(taps.shape[0], out_rows, blocks * block)


def correlate_sum(padded, taps):
    extent = taps.shape[-1]
    out_rows = padded.shape[1] - extent + 1
    out_cols = padded.shape[2] - extent + 1
    block = min(out_cols, 128)
    blocks = -(-out_cols // block)

    def add_channel(total, pair):
        plane, plane_taps = pair
        plane_table = banded_table(plane_taps[None], block)
        patches = patches_of(plane, extent, block, out_rows, out_cols)
        return (
            total
            + jnp.einsum("rnk,kb->rnb", patches, plane_table, preferred_element_type=jnp.float32),
            None,
        )

    start = jnp.zeros((out_rows, blocks, block), jnp.float32)
    total, _ = lax.scan(add_channel, start, (padded, taps))
    return total.reshape(out_rows, blocks * block)


def intensity_of(fields, weights):
    squared = fields * fields
    paired = squared.reshape(weights.shape[0], 2, squared.shape[1], squared.shape[2]).sum(axis=1)
    return jnp.sum(weights[:, None, None] * paired, axis=0)


def body(mask, target, kernels, weights, doses, site_pix, send_count, recv_frag, frag_target):
    tile_rows, tile_cols = mask.shape
    extent = kernels.shape[-1]
    reach = extent // 2
    kernel_taps = kernels.reshape(-1, extent, extent)
    flipped = kernel_taps[:, ::-1, ::-1]
    field_gain = jnp.repeat(weights, 2)
    padded = extended(mask, (("row", 0), ("col", 1)), reach)
    fields = correlate_bank(padded, kernel_taps)
    intensity = intensity_of(fields, weights)
    nominal = jax.nn.sigmoid(steepness * (intensity - threshold))
    dense = (nominal - target.astype(jnp.float32)) * steepness * nominal * (1.0 - nominal)
    devices = site_pix.shape[0]
    slots = site_pix.shape[1]
    conditions = doses.shape[0]
    frag_count = frag_target.shape[1]
    flat_sites = site_pix.reshape(-1)
    level = intensity.reshape(-1)[flat_sites].reshape(devices, slots)
    live = (jnp.arange(slots)[None, :] < send_count[0][:, None]).astype(jnp.float32)
    resist = jax.nn.sigmoid(steepness * (doses[:, None, None] * level[None] - threshold))
    sent_values = resist * live[None]
    owner_frag = recv_frag.reshape(-1)

    def add_sites(values_line):
        return jax.ops.segment_sum(values_line, owner_frag, frag_count)

    arrived = lax.all_to_all(
        sent_values.astype(jnp.bfloat16), ("row", "col"), split_axis=1, concat_axis=1, tiled=True
    ).astype(sent_values.dtype)
    summed = jax.vmap(add_sites)(arrived.reshape(conditions, -1))
    errors = summed - frag_target
    replies = errors[:, owner_frag].reshape(conditions, devices, slots)
    frag_error, replies = (errors, replies)
    returned = lax.all_to_all(replies, ("row", "col"), split_axis=1, concat_axis=1, tiled=True)
    site_terms = returned * live[None] * steepness * doses[:, None, None] * resist * (1.0 - resist)
    site_slope = jnp.sum(site_terms, axis=0)
    slope = (
        dense.reshape(-1).at[flat_sites].add(site_slope.reshape(-1)).reshape(tile_rows, tile_cols)
    )
    weighted = (fields * field_gain[:, None, None] * slope[None]).astype(jnp.bfloat16)
    wide_weighted = extended(weighted, (("row", 1), ("col", 2)), reach)
    gradient = 2.0 * correlate_sum(wide_weighted, flipped)
    return (gradient, frag_error)


def solution(mesh):
    return jax.shard_map(
        body,
        mesh=mesh,
        in_specs=(
            P("row", "col"),
            P("row", "col"),
            P(),
            P(),
            P(),
            P("row", "col"),
            P("row", "col"),
            P("row", "col"),
            P(None, ("row", "col")),
        ),
        out_specs=(P("row", "col"), P(None, ("row", "col"))),
        check_vma=False,
    )
```

profile of v0, /device:TPU:1, one launch (start us, length us, event | category | flops | bytes accessed | tf_op | source)
XLA Modules:
  0.0 1558.8 jit_solution(6779814049358740356)
XLA Ops:
  9.0 16.2 %gather_fusion.1 = bf16[2048,16,33]{2,1,0:T(8,128)(2,1)} fusion(bf16[16,33,33]{1,0,2:T(8,128)(2,1)S(1)} %bitcast.522, s32[2048]{0:T(1024)S(1)} %broadcast_clamp_fusion.2), kind=kCustom, calls=%fused_computation.1 | custom fusion | bytes 4333568 | tf_op jit(solution)/shard_map/gather | solution.py:28
  25.3 12.2 copy.272
  71.1 34.3 %gather_fusion.2 = f32[6144]{0:T(1024)S(1)} fusion(f32[8192]{0:T(1024)S(1)} %bitcast.521, s32[6144]{0:T(1024)S(1)} %get-tuple-element.93), kind=kCustom, calls=%fused_computation.2 | custom fusion | bytes 73728 | tf_op jit(solution)/shard_map/gather | solution.py:101
  106.8 13.6 all-to-all-start
  133.5 33.7 %scatter_custom_fusion = f32[8,2048]{0,1:T(8,128)S(1)} fusion(s32[6144]{0:T(1024)S(1)} %reshape.272, f32[6144,8]{1,0:T(8,128)} %copy.280, f32[]{:T(128)} %constant.24.clone.1), kind=kCustom, calls=%fused_computation.196 | custom fusion | flops 49152 | bytes 66048 | tf_op jit(solution)/shard_map/vmap()/scatter-add | solution.py:108
  167.4 21.0 %gather_fusion.3 = f32[6144,8]{1,0:T(8,128)} fusion(f32[8,2048]{0,1:T(8,128)S(1)} %sub.90, s32[6144]{0:T(1024)S(1)} %get-tuple-element.92), kind=kCustom, calls=%fused_computation.3 | custom fusion | bytes 417792 | tf_op jit(solution)/shard_map/gather | solution.py:115
  209.2 33.4 %scatter_fusion = f32[8192]{0:T(1024)S(1)} fusion(f32[8192]{0:T(1024)S(1)} %bitcast.520, s32[6144]{0:T(1024)S(1)} %bitcast.535, f32[6144]{0:T(1024)S(1)} %reshape.282), kind=kCustom, calls=%fused_computation.5 | custom fusion | flops 6144 | bytes 98304 | tf_op jit(solution)/shard_map/scatter-add | solution.py:121
  261.6 1296.6 %while.11 = (s32[]{:T(128)}, f32[32,2,128]{2,0,1:T(8,128)S(1)}, bf16[16,64,288]{2,1,0:T(8,128)(2,1)S(1)}, bf16[16,33,33]{1,2,0:T(8,128)(2,1)S(1)}, s32[]{:T(128)}, /*index=5*/s32[]{:T(128)}) while((s32[]{:T(128)}, f32[32,2,128]{2,0,1:T(8,128)S(1)}, bf16[16,64,288]{2,1,0:T(8,128)(2,1)S(1)}, bf16[16,33,33]{1,2,0:T(8,128)(2,1)S(1)}, ...), condition=%wide.region_6.7_spmd.clone, body=%wide.region_5.6_spmd.clone.sunk | while | flops 88756224 | bytes 13787519 | solution.py:74
  263.4 72.2 %gather_fusion = bf16[20480,33]{1,0:T(8,128)(2,1)} fusion(bf16[33,33]{0,1:T(8,128)(2,1)S(1)} %dynamic-slice_bitcast_fusion.5, s32[20480]{0:T(1024)S(1)} %fusion.107), kind=kCustom, calls=%fused_computation.clone.clone.1 | custom fusion | bytes 2785280 | tf_op jit(solution)/shard_map/while/body/eval_jaxpr/gather | solution.py:28
  344.4 72.2 %gather_fusion = bf16[20480,33]{1,0:T(8,128)(2,1)} fusion(bf16[33,33]{0,1:T(8,128)(2,1)S(1)} %dynamic-slice_bitcast_fusion.5, s32[20480]{0:T(1024)S(1)} %fusion.107), kind=kCustom, calls=%fused_computation.clone.clone.1 | custom fusion | bytes 2785280 | tf_op jit(solution)/shard_map/while/body/eval_jaxpr/gather | solution.py:28
  425.5 72.2 %gather_fusion = bf16[20480,33]{1,0:T(8,128)(2,1)} fusion(bf16[33,33]{0,1:T(8,128)(2,1)S(1)} %dynamic-slice_bitcast_fusion.5, s32[20480]{0:T(1024)S(1)} %fusion.107), kind=kCustom, calls=%fused_computation.clone.clone.1 | custom fusion | bytes 2785280 | tf_op jit(solution)/shard_map/while/body/eval_jaxpr/gather | solution.py:28
  506.5 72.2 %gather_fusion = bf16[20480,33]{1,0:T(8,128)(2,1)} fusion(bf16[33,33]{0,1:T(8,128)(2,1)S(1)} %dynamic-slice_bitcast_fusion.5, s32[20480]{0:T(1024)S(1)} %fusion.107), kind=kCustom, calls=%fused_computation.clone.clone.1 | custom fusion | bytes 2785280 | tf_op jit(solution)/shard_map/while/body/eval_jaxpr/gather | solution.py:28
  587.5 72.2 %gather_fusion = bf16[20480,33]{1,0:T(8,128)(2,1)} fusion(bf16[33,33]{0,1:T(8,128)(2,1)S(1)} %dynamic-slice_bitcast_fusion.5, s32[20480]{0:T(1024)S(1)} %fusion.107), kind=kCustom, calls=%fused_computation.clone.clone.1 | custom fusion | bytes 2785280 | tf_op jit(solution)/shard_map/while/body/eval_jaxpr/gather | solution.py:28
  668.6 72.2 %gather_fusion = bf16[20480,33]{1,0:T(8,128)(2,1)} fusion(bf16[33,33]{0,1:T(8,128)(2,1)S(1)} %dynamic-slice_bitcast_fusion.5, s32[20480]{0:T(1024)S(1)} %fusion.107), kind=kCustom, calls=%fused_computation.clone.clone.1 | custom fusion | bytes 2785280 | tf_op jit(solution)/shard_map/while/body/eval_jaxpr/gather | solution.py:28
  749.6 72.2 %gather_fusion = bf16[20480,33]{1,0:T(8,128)(2,1)} fusion(bf16[33,33]{0,1:T(8,128)(2,1)S(1)} %dynamic-slice_bitcast_fusion.5, s32[20480]{0:T(1024)S(1)} %fusion.107), kind=kCustom, calls=%fused_computation.clone.clone.1 | custom fusion | bytes 2785280 | tf_op jit(solution)/shard_map/while/body/eval_jaxpr/gather | solution.py:28
  830.6 72.2 %gather_fusion = bf16[20480,33]{1,0:T(8,128)(2,1)} fusion(bf16[33,33]{0,1:T(8,128)(2,1)S(1)} %dynamic-slice_bitcast_fusion.5, s32[20480]{0:T(1024)S(1)} %fusion.107), kind=kCustom, calls=%fused_computation.clone.clone.1 | custom fusion | bytes 2785280 | tf_op jit(solution)/shard_map/while/body/eval_jaxpr/gather | solution.py:28
  911.7 72.2 %gather_fusion = bf16[20480,33]{1,0:T(8,128)(2,1)} fusion(bf16[33,33]{0,1:T(8,128)(2,1)S(1)} %dynamic-slice_bitcast_fusion.5, s32[20480]{0:T(1024)S(1)} %fusion.107), kind=kCustom, calls=%fused_computation.clone.clone.1 | custom fusion | bytes 2785280 | tf_op jit(solution)/shard_map/while/body/eval_jaxpr/gather | solution.py:28
  992.7 72.2 %gather_fusion = bf16[20480,33]{1,0:T(8,128)(2,1)} fusion(bf16[33,33]{0,1:T(8,128)(2,1)S(1)} %dynamic-slice_bitcast_fusion.5, s32[20480]{0:T(1024)S(1)} %fusion.107), kind=kCustom, calls=%fused_computation.clone.clone.1 | custom fusion | bytes 2785280 | tf_op jit(solution)/shard_map/while/body/eval_jaxpr/gather | solution.py:28
  1073.8 72.2 %gather_fusion = bf16[20480,33]{1,0:T(8,128)(2,1)} fusion(bf16[33,33]{0,1:T(8,128)(2,1)S(1)} %dynamic-slice_bitcast_fusion.5, s32[20480]{0:T(1024)S(1)} %fusion.107), kind=kCustom, calls=%fused_computation.clone.clone.1 | custom fusion | bytes 2785280 | tf_op jit(solution)/shard_map/while/body/eval_jaxpr/gather | solution.py:28
  1154.8 72.2 %gather_fusion = bf16[20480,33]{1,0:T(8,128)(2,1)} fusion(bf16[33,33]{0,1:T(8,128)(2,1)S(1)} %dynamic-slice_bitcast_fusion.5, s32[20480]{0:T(1024)S(1)} %fusion.107), kind=kCustom, calls=%fused_computation.clone.clone.1 | custom fusion | bytes 2785280 | tf_op jit(solution)/shard_map/while/body/eval_jaxpr/gather | solution.py:28
  1235.8 72.2 %gather_fusion = bf16[20480,33]{1,0:T(8,128)(2,1)} fusion(bf16[33,33]{0,1:T(8,128)(2,1)S(1)} %dynamic-slice_bitcast_fusion.5, s32[20480]{0:T(1024)S(1)} %fusion.107), kind=kCustom, calls=%fused_computation.clone.clone.1 | custom fusion | bytes 2785280 | tf_op jit(solution)/shard_map/while/body/eval_jaxpr/gather | solution.py:28
  1316.9 72.2 %gather_fusion = bf16[20480,33]{1,0:T(8,128)(2,1)} fusion(bf16[33,33]{0,1:T(8,128)(2,1)S(1)} %dynamic-slice_bitcast_fusion.5, s32[20480]{0:T(1024)S(1)} %fusion.107), kind=kCustom, calls=%fused_computation.clone.clone.1 | custom fusion | bytes 2785280 | tf_op jit(solution)/shard_map/while/body/eval_jaxpr/gather | solution.py:28
  1397.9 72.2 %gather_fusion = bf16[20480,33]{1,0:T(8,128)(2,1)} fusion(bf16[33,33]{0,1:T(8,128)(2,1)S(1)} %dynamic-slice_bitcast_fusion.5, s32[20480]{0:T(1024)S(1)} %fusion.107), kind=kCustom, calls=%fused_computation.clone.clone.1 | custom fusion | bytes 2785280 | tf_op jit(solution)/shard_map/while/body/eval_jaxpr/gather | solution.py:28
  1478.9 72.2 %gather_fusion = bf16[20480,33]{1,0:T(8,128)(2,1)} fusion(bf16[33,33]{0,1:T(8,128)(2,1)S(1)} %dynamic-slice_bitcast_fusion.5, s32[20480]{0:T(1024)S(1)} %fusion.107), kind=kCustom, calls=%fused_computation.clone.clone.1 | custom fusion | bytes 2785280 | tf_op jit(solution)/shard_map/while/body/eval_jaxpr/gather | solution.py:28
  (816 shorter events, 233.2 us)
Async XLA Ops:
  1.3 42.0 %collective-permute-start = (bf16[16,256]{1,0:T(8,128)(2,1)S(1)}, bf16[16,256]{1,0:T(8,128)(2,1)S(1)}, u32[]{:S(2)}, u32[]{:S(2)}) collective-permute-start(bf16[16,256]{1,0:T(8,128)(2,1)S(1)} %get-tuple-element.89), channel_id=1, source_target_pairs={{0,16},{16,32},{32,48},{48,64},{64,80},{80,96},{96,112},{1,17},{17... | collective-permute-start | bytes 24584 | tf_op jit(solution)/shard_map/ppermute | solution.py:15
  5.9 37.5 %collective-permute-start.1 = (bf16[16,256]{1,0:T(8,128)(2,1)S(1)}, bf16[16,256]{1,0:T(8,128)(2,1)S(1)}, u32[]{:S(2)}, u32[]{:S(2)}) collective-permute-start(bf16[16,256]{1,0:T(8,128)(2,1)S(1)} %get-tuple-element.88), channel_id=1, source_target_pairs={{16,0},{32,16},{48,32},{64,48},{80,64},{96,80},{112,96},{17,1},{33... | collective-permute-start | bytes 24584 | tf_op jit(solution)/shard_map/ppermute | solution.py:18
  25.3 12.2 copy-start.5
  25.3 12.5 copy-start.6
  38.0 5.4 copy-start.2
  38.0 8.7 copy-start.9
  43.5 12.0 collective-permute-start.2
  54.2 4.5 collective-permute-start.3
  69.4 1.6 copy-start.8
  71.1 34.5 %copy-start.7 = (f32[8]{0:T(128)S(1)}, f32[8]{0:T(128)}, u32[]{:S(2)}) copy-start(f32[8]{0:T(128)} %param.15) | copy-start | bytes 100
  71.1 49.4 %copy-start.1 = (f32[8,2048]{1,0:T(8,128)S(1)}, f32[8,2048]{1,0:T(8,128)}, u32[]{:S(2)}) copy-start(f32[8,2048]{1,0:T(8,128)} %param.19) | copy-start | bytes 196612
  106.8 23.8 %all-to-all-start = ((bf16[128,2,192]{2,1,0:T(2,128)(2,1)}), bf16[128,2,192]{2,1,0:T(2,128)(2,1)S(1)}, u32[]{:S(2)}, u32[]{:S(2)}) async-start(bf16[128,2,192]{2,1,0:T(2,128)(2,1)} %reshape.302), calls=%async_computation | async-start | bytes 262144 | tf_op jit(solution)/shard_map/all_to_all | solution.py:110
  188.4 7.5 copy-start.3
  192.0 14.8 all-to-all-start.1
  209.2 33.4 %copy-start = (f32[16,32,256]{2,0,1:T(8,128)S(1)}, f32[16,32,256]{2,0,1:T(8,128)}, u32[]{:S(2)}) copy-start(f32[16,32,256]{2,0,1:T(8,128)} %reshape.226) | copy-start | bytes 1572868
  243.0 6.3 collective-permute-start.5
  245.4 5.1 collective-permute-start.4
  250.7 8.7 collective-permute-start.7
  252.0 9.1 collective-permute-start.6
  262.3 1.0 copy-start.4
  343.4 1.0 copy-start.4
  424.4 1.0 copy-start.4
  505.4 1.0 copy-start.4
  586.5 1.0 copy-start.4
  (11 other events, 11.3 us)
where the time goes:
time: 1560 us
  local copies, waits for them, and re-layouts  1370 us (88%)
  other arithmetic  85.1 us (5%)
  starting transfers between devices  39.3 us (3%)
  matrix products  32.9 us (2%)
  waiting for transfers between devices  26 us (2%)
    gather x34, local copies, waits for them, and re-layouts, banded_table(): picked = taps[:, :, jnp.clip(offsets, 0, extent - 1)]  1270 us
    gather x1, local copies, waits for them, and re-layouts, body(): level = intensity.reshape(-1)[flat_sites].reshape(devices, slots)  34.3 us
    scatter-add x1, other arithmetic, add_sites(): return jax.ops.segment_sum(values_line, owner_frag, frag_count)  33.7 us
    scatter-add x1, other arithmetic, body(): dense.reshape(-1).at[flat_sites].add(site_slope.reshape(-1))  33.4 us
  transfers between devices with their start and end apart: 10, of which 7 were waited for; matrix products, arithmetic and copies ran while one was open for 3% of the time, Pallas kernels for 0%

commit v1 on v0

v1 whole, which is shorter than its diff:
```python
import functools

import jax
import jax.numpy as jnp
from jax import lax
from jax.experimental import pallas as pl
from jax.experimental.pallas import tpu as pltpu
from jax.sharding import PartitionSpec as P

steepness = 4.0
threshold = 1.2
f32 = jnp.float32
bf16 = jnp.bfloat16
LANES = 128
VMEM_BYTES = 48 << 20


def call(kernel, out_shapes, scratch=(), flops=0, moved=0, smem=(), inputs=0):
    vmem = pl.BlockSpec(memory_space=pltpu.VMEM)
    specs = [
        pl.BlockSpec(memory_space=pltpu.SMEM) if i in smem else vmem for i in range(inputs)
    ]
    return pl.pallas_call(
        kernel,
        out_shape=out_shapes,
        in_specs=specs,
        out_specs=jax.tree.map(lambda _: vmem, out_shapes),
        scratch_shapes=list(scratch),
        cost_estimate=pl.CostEstimate(flops=flops, bytes_accessed=moved, transcendentals=0),
        compiler_params=pltpu.CompilerParams(vmem_limit_bytes=VMEM_BYTES),
    )


def ring_halo(block, axis, dim, width):
    count = lax.axis_size(axis)
    index = lax.axis_index(axis)
    up = [(i, (i + 1) % count) for i in range(count)]
    down = [(target, source) for source, target in up]
    size = block.shape[dim]
    low = lax.ppermute(lax.slice_in_dim(block, size - width, size, axis=dim), axis, up)
    high = lax.ppermute(lax.slice_in_dim(block, 0, width, axis=dim), axis, down)
    zero = jnp.zeros((), block.dtype)
    low = jnp.where(index == 0, zero, low)
    high = jnp.where(index == count - 1, zero, high)
    return jnp.concatenate([low, block, high], axis=dim)


def shear(row, rows):
    wide = jnp.broadcast_to(row, (rows, row.shape[1]))
    return pltpu.roll(wide, 0, axis=1, stride=1, stride_axis=0)


def table_kernel(rows, lines_ref, out_ref):
    def one(index, carry):
        line = lines_ref[pl.ds(index, 1), :]
        start = pl.multiple_of(index * rows, rows)
        out_ref[pl.ds(start, rows), :] = shear(line, rows).astype(bf16)
        return carry

    lax.fori_loop(0, lines_ref.shape[0], one, 0)


def banded(lines, rows):
    count, width = lines.shape
    return call(
        functools.partial(table_kernel, rows),
        jax.ShapeDtypeStruct((count * rows, width), bf16),
        inputs=1,
        moved=2 * count * rows * width,
    )(lines)


def stack_shifts(plane, taps, first, out_ref):
    height, width = plane.shape
    columns = out_ref.shape[1]

    def one(v, carry):
        moved = pltpu.roll(plane, width - first - v, axis=1)[:, :columns]
        start = pl.multiple_of(v * height, height)
        out_ref[pl.ds(start, height), :] = moved.astype(bf16)
        return carry

    lax.fori_loop(0, taps, one, 0)
    rest = out_ref.shape[0] - taps * height
    out_ref[taps * height :, :] = jnp.zeros((rest, columns), bf16)


def forward_kernel(
    taps, reach, gain_ref, mask_ref, table_ref, pix_ref, count_ref, level_ref, inten_ref, stack_ref, lines_ref
):
    rows, columns = inten_ref.shape
    plane = mask_ref[reach : reach + rows + 2 * reach, :].astype(f32)
    stack_shifts(plane, taps, reach, stack_ref)
    fields = jnp.dot(table_ref[...], stack_ref[...], preferred_element_type=f32)
    total = jnp.zeros((rows, columns), f32)
    for k in range(gain_ref.shape[0]):
        real = fields[2 * k * rows : (2 * k + 1) * rows]
        imag = fields[(2 * k + 1) * rows : (2 * k + 2) * rows]
        total = total + gain_ref[k] * (real * real + imag * imag)
    inten_ref[...] = total
    halves = columns // LANES
    for half in range(halves):
        lines_ref[half * rows : (half + 1) * rows, :] = total[:, half * LANES : (half + 1) * LANES]
    pix = pix_ref[...]
    slots, owners = pix.shape
    low = pix & (LANES - 1)
    high = pix >> 7

    def pick(i, level):
        for half in range(halves):
            line = lines_ref[pl.ds(half * rows + i, 1), :]
            wide = jnp.broadcast_to(line, (slots, LANES))
            found = jnp.take_along_axis(wide, low, axis=1, mode="promise_in_bounds")
            level = jnp.where(high == i * halves + half, found, level)
        return level

    level = lax.fori_loop(0, rows, pick, jnp.zeros((slots, owners), f32))
    live = lax.broadcasted_iota(jnp.int32, (slots, owners), 0) < count_ref[...]
    level = jnp.where(live, level, -1.0)
    level = jnp.concatenate([level, jnp.zeros((owners - slots, owners), f32)], axis=0)
    level_ref[...] = level.T


def wide_kernel(taps, rows, chunk, mask_ref, lines_ref, fields_ref, table_ref, stack_ref):
    plane = mask_ref[...].astype(f32)
    stack_shifts(plane, taps, 0, stack_ref)
    table_kernel(rows, lines_ref, table_ref)
    count = table_ref.shape[0] // chunk

    def one(index, carry):
        start = pl.multiple_of(index * chunk, chunk)
        fields_ref[pl.ds(start, chunk), :] = jnp.dot(
            table_ref[pl.ds(start, chunk), :], stack_ref[...], preferred_element_type=f32
        )
        return carry

    lax.fori_loop(0, count, one, 0)


def split(x):
    top = x.astype(bf16)
    return top.astype(f32), x - top.astype(f32)


def one_hot(index, size):
    ids = lax.broadcasted_iota(jnp.int32, (size, LANES), 0)
    return jnp.where(ids == index, 1.0, 0.0).astype(bf16)


def product_nt(a, b):
    return lax.dot_general(a, b, (((1,), (1,)), ((), ())), preferred_element_type=f32)


def owner_kernel(dose_ref, level_ref, frag_ref, aim_ref, error_ref, slope_ref, level_t, slope_t):
    slots = frag_ref.shape[0]
    conds = dose_ref.shape[0]
    bins = aim_ref.shape[1] // LANES
    level_t[...] = level_ref[...].T
    dose = jnp.broadcast_to(dose_ref[...], (conds, LANES))

    def resist_of(c):
        level = jnp.broadcast_to(level_t[pl.ds(c, 1), :], (conds, LANES))
        return level, jax.nn.sigmoid(steepness * (dose * level - threshold))

    def add(pair, total):
        left, right = [], []
        for c in (2 * pair, 2 * pair + 1):
            level, resist = resist_of(c)
            frag = jnp.broadcast_to(frag_ref[pl.ds(c, 1), :], (conds, LANES))
            top, rest = split(jnp.where(level >= 0.0, resist, 0.0))
            bin_of = frag >> 7
            left.append(
                jnp.concatenate(
                    [jnp.where(bin_of == q, part, 0.0) for part in (top, rest) for q in range(bins)],
                    axis=0,
                ).astype(bf16)
            )
            right.append(one_hot(frag_ref[pl.ds(c, 1), :] & (LANES - 1), LANES))
        return total + product_nt(
            jnp.concatenate(left, axis=1), jnp.concatenate(right, axis=1)
        )

    total = lax.fori_loop(0, slots // 2, add, jnp.zeros((2 * bins * conds, LANES), f32))
    total = total[: bins * conds] + total[bins * conds :]
    for q in range(bins):
        lanes = slice(q * LANES, (q + 1) * LANES)
        error_ref[:, lanes] = total[q * conds : (q + 1) * conds] - aim_ref[:, lanes]

    def answer(c, carry):
        level, resist = resist_of(c)
        frag = jnp.broadcast_to(frag_ref[pl.ds(c, 1), :], (conds, LANES))
        low = frag & (LANES - 1)
        bin_of = frag >> 7
        reply = jnp.zeros((conds, LANES), f32)
        for q in range(bins):
            found = jnp.take_along_axis(
                error_ref[:, q * LANES : (q + 1) * LANES], low, axis=1, mode="promise_in_bounds"
            )
            reply = jnp.where(bin_of == q, found, reply)
        terms = reply * steepness * dose * resist * (1.0 - resist)
        terms = jnp.where(level >= 0.0, terms, 0.0)
        slope_t[pl.ds(c, 1), :] = jnp.sum(terms, axis=0, keepdims=True)
        return carry

    lax.fori_loop(0, slots, answer, 0)
    slope_t[slots:, :] = jnp.zeros((LANES - slots, LANES), f32)
    slope_ref[...] = slope_t[...].T


def site_kernel(reply_ref, pix_ref, inten_ref, target_ref, slope_ref, reply_t):
    rows, columns = inten_ref.shape
    slots = pix_ref.shape[0]
    halves = columns // LANES
    reply_t[...] = reply_ref[...].T

    def add(pair, total):
        left, right = [], []
        for c in (2 * pair, 2 * pair + 1):
            pix = pix_ref[pl.ds(c, 1), :]
            line = pix >> 7
            line = (line % halves) * rows + line // halves
            ids = lax.broadcasted_iota(jnp.int32, (rows * halves, LANES), 0)
            top, rest = split(reply_t[pl.ds(c, 1), :])
            here = ids == line
            left.append(
                jnp.concatenate(
                    [jnp.where(here, top, 0.0), jnp.where(here, rest, 0.0)], axis=0
                ).astype(bf16)
            )
            right.append(one_hot(pix & (LANES - 1), LANES))
        return total + product_nt(
            jnp.concatenate(left, axis=1), jnp.concatenate(right, axis=1)
        )

    size = rows * halves
    total = lax.fori_loop(0, slots // 2, add, jnp.zeros((2 * size, LANES), f32))
    total = total[:size] + total[size:]
    for half in range(halves):
        lanes = slice(half * LANES, (half + 1) * LANES)
        nominal = jax.nn.sigmoid(steepness * (inten_ref[:, lanes] - threshold))
        gap = nominal - target_ref[:, lanes].astype(f32)
        dense = gap * steepness * nominal * (1.0 - nominal)
        slope_ref[:, lanes] = dense + total[half * rows : (half + 1) * rows]


def back_kernel(taps, gain_ref, fields_ref, slope_ref, table_ref, out_ref, weighted_ref, part_ref):
    rows, columns = out_ref.shape
    height, width = slope_ref.shape
    slope = slope_ref[...]

    def weigh(h, carry):
        start = pl.multiple_of(h * height, height)
        field = fields_ref[pl.ds(start, height), :]
        weighted_ref[pl.ds(start, height), :] = (gain_ref[h // 2] * field * slope).astype(bf16)
        return carry

    lax.fori_loop(0, weighted_ref.shape[0] // height, weigh, 0)
    part_ref[...] = jnp.dot(table_ref[...], weighted_ref[...], preferred_element_type=f32)

    def gather(v, total):
        start = pl.multiple_of(v * rows, rows)
        return total + pltpu.roll(part_ref[pl.ds(start, rows), :], width - v, axis=1)[:, :columns]

    total = lax.fori_loop(0, taps, gather, jnp.zeros((rows, columns), f32))
    out_ref[...] = 2.0 * total


def round_up(x, to):
    return -(-x // to) * to


def lines_of(taps, stride, length):
    count, blocks, extent = taps.shape
    padded = jnp.pad(taps, ((0, 0), (0, 0), (0, stride - extent)))
    flat = padded.reshape(count, blocks * stride)
    return jnp.pad(flat, ((0, 0), (0, length - blocks * stride))).astype(f32)


def body(mask, target, kernels, weights, doses, site_pix, send_count, recv_frag, frag_target):
    rows, columns = mask.shape
    extent = kernels.shape[-1]
    reach = extent // 2
    kernel_taps = kernels.reshape(-1, extent, extent)
    parts = kernel_taps.shape[0]
    owners = site_pix.shape[0]
    both = ("row", "col")

    near = ring_halo(mask, "row", 0, 2 * reach)
    near = ring_halo(near, "col", 1, 2 * reach)
    wide_columns = round_up(near.shape[1], LANES)
    near = jnp.pad(near, ((0, 0), (0, wide_columns - near.shape[1])))

    height = rows + 2 * reach
    by_column = kernel_taps.transpose(0, 2, 1)
    core_depth = round_up(extent * height, LANES)
    core_table = banded(lines_of(by_column, height, core_depth), rows)

    pix = site_pix.T
    level, intensity = call(
        functools.partial(forward_kernel, extent, reach),
        (
            jax.ShapeDtypeStruct((owners, LANES), f32),
            jax.ShapeDtypeStruct((rows, columns), f32),
        ),
        scratch=[
            pltpu.VMEM((core_depth, columns), bf16),
            pltpu.VMEM((rows * columns // LANES, LANES), f32),
        ],
        inputs=5,
        smem=(0,),
        flops=2 * parts * rows * core_depth * columns,
        moved=2 * parts * rows * core_depth,
    )(weights, near, core_table, pix, send_count)

    level, near = lax.optimization_barrier((level, near))
    arrived = lax.all_to_all(level, both, split_axis=0, concat_axis=0, tiled=True)

    tall = rows + 4 * reach
    wide_depth = round_up(extent * tall, LANES)
    wide_fields = call(
        functools.partial(wide_kernel, extent, height, 256),
        jax.ShapeDtypeStruct((parts * height, wide_columns), f32),
        scratch=[
            pltpu.VMEM((parts * height, wide_depth), bf16),
            pltpu.VMEM((wide_depth, wide_columns), bf16),
        ],
        inputs=2,
        flops=2 * parts * height * wide_depth * wide_columns,
        moved=4 * parts * height * wide_columns,
    )(near, lines_of(by_column, tall, wide_depth))

    arrived, wide_fields = lax.optimization_barrier((arrived, wide_fields))

    frag_error, answers = call(
        owner_kernel,
        (
            jax.ShapeDtypeStruct(frag_target.shape, f32),
            jax.ShapeDtypeStruct((owners, LANES), f32),
        ),
        scratch=[pltpu.VMEM((LANES, LANES), f32)] * 2,
        inputs=4,
        flops=2 * 2 * frag_target.size * site_pix.size // 16,
        moved=8 * frag_target.size,
    )(doses[:, None], arrived, recv_frag.T, frag_target)

    flipped = kernel_taps[:, ::-1, ::-1].transpose(2, 0, 1)
    back_depth = parts * height
    back_lines = lines_of(flipped, height, back_depth)
    answers, back_lines = lax.optimization_barrier((answers, back_lines))
    returned = lax.all_to_all(answers, both, split_axis=0, concat_axis=0, tiled=True)
    back_table = banded(back_lines, rows)
    returned, back_table = lax.optimization_barrier((returned, back_table))
    slope = call(
        site_kernel,
        jax.ShapeDtypeStruct((rows, columns), f32),
        scratch=[pltpu.VMEM((LANES, LANES), f32)],
        inputs=4,
        flops=2 * 2 * rows * columns * site_pix.size // 64,
        moved=16 * rows * columns,
    )(returned, pix, intensity, target)

    around = ring_halo(slope, "row", 0, reach)
    around = ring_halo(around, "col", 1, reach)
    around = jnp.pad(around, ((0, 0), (0, wide_columns - around.shape[1])))
    gradient = call(
        functools.partial(back_kernel, extent),
        jax.ShapeDtypeStruct((rows, columns), f32),
        scratch=[
            pltpu.VMEM((back_depth, wide_columns), bf16),
            pltpu.VMEM((extent * rows, wide_columns), f32),
        ],
        inputs=4,
        smem=(0,),
        flops=2 * extent * rows * back_depth * wide_columns,
        moved=8 * back_depth * wide_columns,
    )(weights, wide_fields, around, back_table)
    return gradient, frag_error


def solution(mesh):
    return jax.shard_map(
        body,
        mesh=mesh,
        in_specs=(
            P("row", "col"),
            P("row", "col"),
            P(),
            P(),
            P(),
            P("row", "col"),
            P("row", "col"),
            P("row", "col"),
            P(None, ("row", "col")),
        ),
        out_specs=(P("row", "col"), P(None, ("row", "col"))),
        check_vma=False,
    )
```

time: 1560 us -> 98.2 us (0.06)
  local copies, waits for them, and re-layouts: 1370 us -> 5.01 us
  other arithmetic: 85.1 us -> 0.3 us
  Pallas kernels: 0 us -> 43.8 us
  matrix products: 32.9 us -> 0 us
    gather x36 -> x0, local copies, waits for them, and re-layouts: 1320 us -> none  [the longest x34 1270 us: banded_table(): picked = taps[:, :, jnp.clip(offsets, 0, extent - 1)]]
    scatter-add x2 -> x0, other arithmetic: 67.1 us -> none  [the longest x1 33.7 us: add_sites(): return jax.ops.segment_sum(values_line, owner_frag, frag_count)]
    pallas_call x0 -> x7, Pallas kernels: none -> 43.8 us  [the longest x1 10.7 us: body(): call(functools.partial(wide_kernel, extent, height, 256), jax.ShapeDtypeS...]
    dot_general x17 -> x0, matrix products: 32.9 us -> none  [the longest x16 27 us: add_channel(): jnp.einsum('rnk,kb->rnb', patches, plane_table, preferred_element_type=jn...]
    reshape x9 -> x3, local copies, waits for them, and re-layouts: 17.5 us -> 0.55 us  [the longest x2 0.29 us: lines_of(): flat = padded.reshape(count, blocks * stride)]
    while x32 -> x0, local copies, waits for them, and re-layouts: 16.3 us -> none
  transfers between devices with their start and end apart: 10 -> 10, of which waited for: 7 -> 6; matrix products, arithmetic and copies ran while one was open for 3% -> 2% of each run, Pallas kernels for 0% -> 16%
where the time goes in v1:
time: 98.2 us; the launch traced here: 97.5 us
  Pallas kernels  43.8 us (45%)
  starting transfers between devices  33.8 us (34%)
  waiting for transfers between devices  13.6 us (14%)
  local copies, waits for them, and re-layouts  5.01 us (5%)
    pallas_call x1, Pallas kernels, body(): call(functools.partial(wide_kernel, extent, height, 256), jax.ShapeDtypeS...  10.7 us
    pallas_call x1, Pallas kernels, body(): call(owner_kernel, (jax.ShapeDtypeStruct(frag_target.shape, f32), jax.Sha...  10.3 us
    all_to_all x1, starting transfers between devices, body(): lax.all_to_all(answers, both, split_axis=0, concat_axis=0, tiled=True)  9.76 us
    ppermute x4, starting transfers between devices, ring_halo(): high = lax.ppermute(lax.slice_in_dim(block, 0, width, axis=dim), axis, down)  9.43 us
    all_to_all x1, starting transfers between devices, body(): lax.all_to_all(level, both, split_axis=0, concat_axis=0, tiled=True)  9.31 us
    pallas_call x1, Pallas kernels, body(): call(functools.partial(forward_kernel, extent, reach), (jax.ShapeDtypeStr...  8.22 us
    all_to_all x1, waiting for transfers between devices, body(): lax.all_to_all(answers, both, split_axis=0, concat_axis=0, tiled=True)  6.72 us
    pallas_call x1, Pallas kernels, body(): call(functools.partial(back_kernel, extent), jax.ShapeDtypeStruct((rows,...  5.61 us
  transfers between devices with their start and end apart: 10, of which 6 were waited for; matrix products, arithmetic and copies ran while one was open for 2% of the time, Pallas kernels for 16%

profile of v1, /device:TPU:1, one launch (start us, length us, event | category | flops | bytes accessed | tf_op | source)
XLA Modules:
  0.0 97.5 jit_solution(12676623133457355357)
XLA Ops:
  0.6 2.6 %collective-permute-start = (bf16[32,256]{1,0:T(8,128)(2,1)}, bf16[32,256]{1,0:T(8,128)(2,1)S(1)}, u32[]{:S(2)}, u32[]{:S(2)}) collective-permute-start(bf16[32,256]{1,0:T(8,128)(2,1)} %param.9), channel_id=1, source_target_pairs={{0,16},{16,32},{32,48},{48,64},{64,80},{80,96},{96,112},{112,0},{1... | collective-permute-start | bytes 49160 | tf_op jit(solution)/shard_map/ppermute | solution.py:40
  3.3 1.0 %copy.26 = bf16[8,2,33,33]{3,1,0,2:T(2,128)(2,1)S(1)} copy(bf16[8,2,33,33]{3,1,2,0:T(2,128)(2,1)} %param.11) | data formatting | bytes 69696 | tf_op args[2]
  5.4 1.2 %collective-permute-done.1 = bf16[32,256]{1,0:T(8,128)(2,1)S(1)} collective-permute-done((bf16[32,256]{1,0:T(8,128)(2,1)}, bf16[32,256]{1,0:T(8,128)(2,1)S(1)}, u32[]{:S(2)}, u32[]{:S(2)}) %collective-permute-start.1) | collective-permute-done | bytes 16416 | tf_op jit(solution)/shard_map/ppermute | solution.py:41
  6.7 1.3 %collective-permute-start.2 = (bf16[96,32]{1,0:T(8,128)(2,1)S(1)}, bf16[96,32]{1,0:T(8,128)(2,1)S(1)}, u32[]{:S(2)}, u32[]{:S(2)}) collective-permute-start(bf16[96,32]{1,0:T(8,128)(2,1)S(1)} %get-tuple-element.28), channel_id=1, source_target_pairs={{0,1},{1,2},{2,3},{3,4},{4,5},{5,6},{6,7},{7,8},{8,9},{9,10},{10,1... | collective-permute-start | bytes 18440 | tf_op jit(solution)/shard_map/ppermute | solution.py:40
  8.3 1.8 %shard_map.104.table_ref = bf16[512,2176]{1,0:T(8,128)(2,1)S(1)} custom-call(f32[16,2176]{1,0:T(8,128)S(1)} %pad_convert_fusion.2.lines_ref), custom_call_target="tpu_custom_call" | custom-call | bytes 2228224 | tf_op jit(solution)/shard_map/pallas_call | solution.py:65
  10.1 5.0 %collective-permute-start.3 = (bf16[96,32]{1,0:T(8,128)(2,1)S(1)}, bf16[96,32]{1,0:T(8,128)(2,1)S(1)}, u32[]{:S(2)}, u32[]{:S(2)}) collective-permute-start(bf16[96,32]{1,0:T(8,128)(2,1)S(1)} %get-tuple-element.29), channel_id=1, source_target_pairs={{1,0},{2,1},{3,2},{4,3},{5,4},{6,5},{7,6},{8,7},{9,8},{10,9},{11,1... | collective-permute-start | bytes 18440 | tf_op jit(solution)/shard_map/ppermute | solution.py:41
  15.1 0.9 collective-permute-done.3
  16.2 8.2 %shard_map.105 = (f32[128,128]{1,0:T(8,128)}, f32[32,256]{1,0:T(8,128)S(1)}) custom-call(f32[8]{0:T(128)S(1)} %copy-done.6, bf16[96,384]{1,0:T(8,128)(2,1)S(1)} %fusion.11.mask_ref, bf16[512,2176]{1,0:T(8,128)(2,1)S(1)} %shard_map.104.table_ref, s32[48,128]{1,0:T(8,128)S(1)} %bitcast.17, s32[1,128]{1,0:T(1,128)S(1)} %copy-done.7), custom_call_target="tpu_custom_call" | custom-call | flops 570425344 | bytes 2228224 | tf_op jit(solution)/shard_map/pallas_call | solution.py:299
  24.4 9.3 %all-to-all-start = ((f32[128,1,128]{2,1,0:T(1,128)}), f32[128,1,128]{2,1,0:T(1,128)S(1)}, u32[]{:S(2)}, u32[]{:S(2)}) async-start(f32[128,1,128]{2,1,0:T(1,128)} %bitcast.4), calls=%async_computation | async-start | bytes 131072 | tf_op jit(solution)/shard_map/all_to_all | solution.py:316
  33.8 10.7 %shard_map.106.fields_ref = f32[1024,384]{1,0:T(8,128)S(1)} custom-call(bf16[96,384]{1,0:T(8,128)(2,1)S(1)} %fusion.11.mask_ref, f32[16,3200]{1,0:T(8,128)S(1)} %pad_convert_fusion.1.lines_ref), custom_call_target="tpu_custom_call" | custom-call | flops 2516582400 | bytes 1572864 | tf_op jit(solution)/shard_map/pallas_call | solution.py:320
  44.5 1.2 %copy-done = f32[1024,384]{1,0:T(8,128)} copy-done((f32[1024,384]{1,0:T(8,128)}, f32[1024,384]{1,0:T(8,128)S(1)}, u32[]{:S(2)}) %copy-start) | copy-done | bytes 1572888
  45.6 10.3 %shard_map.107 = (f32[8,2048]{1,0:T(8,128)}, f32[128,128]{1,0:T(8,128)}) custom-call(f32[8,1]{1,0:T(8,128)S(1)} %copy.30.dose_ref, f32[128,128]{1,0:T(8,128)S(1)} %bitcast.16, s32[48,128]{1,0:T(8,128)S(1)} %bitcast.19, f32[8,2048]{1,0:T(8,128)S(1)} %copy-done.3), custom_call_target="tpu_custom_call" | custom-call | flops 25165824 | bytes 131072 | tf_op jit(solution)/shard_map/pallas_call | solution.py:334
  56.0 9.8 %all-to-all-start.1 = ((f32[128,1,128]{2,1,0:T(1,128)}), f32[128,1,128]{2,1,0:T(1,128)S(1)}, u32[]{:S(2)}, u32[]{:S(2)}) async-start(f32[128,1,128]{2,1,0:T(1,128)} %bitcast.11), calls=%async_computation.1 | async-start | bytes 131072 | tf_op jit(solution)/shard_map/all_to_all | solution.py:350
  65.8 3.0 %shard_map.108.table_ref = bf16[1056,1024]{1,0:T(8,128)(2,1)S(1)} custom-call(f32[33,1024]{1,0:T(8,128)S(1)} %reshape.23.lines_ref), custom_call_target="tpu_custom_call" | custom-call | bytes 2162688 | tf_op jit(solution)/shard_map/pallas_call | solution.py:65
  68.8 6.7 %all-to-all-done.1 = f32[128,1,128]{2,1,0:T(1,128)S(1)} async-done(((f32[128,1,128]{2,1,0:T(1,128)}), f32[128,1,128]{2,1,0:T(1,128)S(1)}, u32[]{:S(2)}, u32[]{:S(2)}) %all-to-all-start.1) | async-done | bytes 65568 | tf_op jit(solution)/shard_map/all_to_all | solution.py:350
  75.5 4.2 %shard_map.109 = f32[32,256]{1,0:T(8,128)S(1)} custom-call(f32[128,128]{1,0:T(8,128)S(1)} %bitcast.15, s32[48,128]{1,0:T(8,128)S(1)} %bitcast.18, f32[32,256]{1,0:T(8,128)S(1)} %get-tuple-element.23.inten_ref, s32[32,256]{1,0:T(8,128)S(1)} %copy-done.4), custom_call_target="tpu_custom_call" | custom-call | flops 3145728 | bytes 131072 | tf_op jit(solution)/shard_map/pallas_call | solution.py:353
  79.7 1.0 %collective-permute-start.4 = (f32[16,256]{1,0:T(8,128)S(1)}, f32[16,256]{1,0:T(8,128)S(1)}, u32[]{:S(2)}, u32[]{:S(2)}) collective-permute-start(f32[16,256]{1,0:T(8,128)S(1)} %get-tuple-element.30), channel_id=1, source_target_pairs={{0,16},{16,32},{32,48},{48,64},{64,80},{80,96},{96,112},{112,0},{1... | collective-permute-start | bytes 49160 | tf_op jit(solution)/shard_map/ppermute | solution.py:40
  80.7 0.9 collective-permute-done.4
  81.6 2.6 %collective-permute-done.5 = f32[16,256]{1,0:T(8,128)S(1)} collective-permute-done((f32[16,256]{1,0:T(8,128)S(1)}, f32[16,256]{1,0:T(8,128)S(1)}, u32[]{:S(2)}, u32[]{:S(2)}) %collective-permute-start.5) | collective-permute-done | bytes 16416 | tf_op jit(solution)/shard_map/ppermute | solution.py:41
  84.2 0.4 collective-permute-start.6
  84.6 4.4 %collective-permute-start.7 = (f32[64,16]{1,0:T(8,128)S(1)}, f32[64,16]{1,0:T(8,128)S(1)}, u32[]{:S(2)}, u32[]{:S(2)}) collective-permute-start(f32[64,16]{1,0:T(8,128)S(1)} %get-tuple-element.27), channel_id=1, source_target_pairs={{1,0},{2,1},{3,2},{4,3},{5,4},{6,5},{7,6},{8,7},{9,8},{10,9},{11,1... | collective-permute-start | bytes 12296 | tf_op jit(solution)/shard_map/ppermute | solution.py:41
  89.0 1.3 %collective-permute-done.6 = f32[64,16]{1,0:T(8,128)S(1)} collective-permute-done((f32[64,16]{1,0:T(8,128)S(1)}, f32[64,16]{1,0:T(8,128)S(1)}, u32[]{:S(2)}, u32[]{:S(2)}) %collective-permute-start.6) | collective-permute-done | bytes 4128 | tf_op jit(solution)/shard_map/ppermute | solution.py:40
  90.5 1.4 %copy-done.1 = f32[1024,384]{1,0:T(8,128)S(1)} copy-done((f32[1024,384]{1,0:T(8,128)S(1)}, f32[1024,384]{1,0:T(8,128)}, u32[]{:S(2)}) %copy-start.1) | copy-done | bytes 1572888
  91.9 5.6 %shard_map.110 = f32[32,256]{1,0:T(8,128)} custom-call(f32[8]{0:T(128)S(1)} %copy-done.6, f32[1024,384]{1,0:T(8,128)S(1)} %copy-done.1, f32[64,384]{1,0:T(8,128)S(1)} %select_maximum_fusion.slope_ref, bf16[1056,1024]{1,0:T(8,128)(2,1)S(1)} %shard_map.108.table_ref), custom_call_target="tpu_custom_call" | custom-call | flops 830472192 | bytes 3145728 | tf_op jit(solution)/shard_map/pallas_call | solution.py:365
  (51 shorter events, 1.8 us)
Async XLA Ops:
  0.6 6.0 %copy-start.8 = (bf16[32,256]{1,0:T(8,128)(2,1)S(1)}, bf16[32,256]{1,0:T(8,128)(2,1)}, u32[]{:S(2)}) copy-start(bf16[32,256]{1,0:T(8,128)(2,1)} %param.9) | copy-start | bytes 49156
  0.6 7.4 %copy-start.9 = (f32[8]{0:T(128)S(1)}, f32[8]{0:T(128)}, u32[]{:S(2)}) copy-start(f32[8]{0:T(128)} %param.13) | copy-start | bytes 100
  0.6 4.8 %collective-permute-start = (bf16[32,256]{1,0:T(8,128)(2,1)}, bf16[32,256]{1,0:T(8,128)(2,1)S(1)}, u32[]{:S(2)}, u32[]{:S(2)}) collective-permute-start(bf16[32,256]{1,0:T(8,128)(2,1)} %param.9), channel_id=1, source_target_pairs={{0,16},{16,32},{32,48},{48,64},{64,80},{80,96},{96,112},{112,0},{1... | collective-permute-start | bytes 49160 | tf_op jit(solution)/shard_map/ppermute | solution.py:40
  3.3 3.4 %collective-permute-start.1 = (bf16[32,256]{1,0:T(8,128)(2,1)}, bf16[32,256]{1,0:T(8,128)(2,1)S(1)}, u32[]{:S(2)}, u32[]{:S(2)}) collective-permute-start(bf16[32,256]{1,0:T(8,128)(2,1)} %param.9), channel_id=1, source_target_pairs={{16,0},{32,16},{48,32},{64,48},{80,64},{96,80},{112,96},{0,112},{1... | collective-permute-start | bytes 49160 | tf_op jit(solution)/shard_map/ppermute | solution.py:41
  5.0 11.2 %copy-start.2 = (s32[128,48]{0,1:T(8,128)S(1)}, s32[128,48]{0,1:T(8,128)}, u32[]{:S(2)}) copy-start(s32[128,48]{0,1:T(8,128)} %param.14) | copy-start | bytes 73732
  5.0 11.2 %copy-start.6 = (f32[8]{0:T(128)S(1)}, f32[8]{0:T(128)}, u32[]{:S(2)}) copy-start(f32[8]{0:T(128)} %gain_ref.3) | copy-start | bytes 100
  5.0 11.2 %copy-start.7 = (s32[1,128]{1,0:T(1,128)S(1)}, s32[1,128]{1,0:T(1,128)}, u32[]{:S(2)}) copy-start(s32[1,128]{1,0:T(1,128)} %count_ref.1) | copy-start | bytes 1540
  6.7 8.4 %collective-permute-start.2 = (bf16[96,32]{1,0:T(8,128)(2,1)S(1)}, bf16[96,32]{1,0:T(8,128)(2,1)S(1)}, u32[]{:S(2)}, u32[]{:S(2)}) collective-permute-start(bf16[96,32]{1,0:T(8,128)(2,1)S(1)} %get-tuple-element.28), channel_id=1, source_target_pairs={{0,1},{1,2},{2,3},{3,4},{4,5},{5,6},{6,7},{7,8},{8,9},{9,10},{10,1... | collective-permute-start | bytes 18440 | tf_op jit(solution)/shard_map/ppermute | solution.py:40
  10.1 5.9 %collective-permute-start.3 = (bf16[96,32]{1,0:T(8,128)(2,1)S(1)}, bf16[96,32]{1,0:T(8,128)(2,1)S(1)}, u32[]{:S(2)}, u32[]{:S(2)}) collective-permute-start(bf16[96,32]{1,0:T(8,128)(2,1)S(1)} %get-tuple-element.29), channel_id=1, source_target_pairs={{1,0},{2,1},{3,2},{4,3},{5,4},{6,5},{7,6},{8,7},{9,8},{10,9},{11,1... | collective-permute-start | bytes 18440 | tf_op jit(solution)/shard_map/ppermute | solution.py:41
  24.4 21.2 %all-to-all-start = ((f32[128,1,128]{2,1,0:T(1,128)}), f32[128,1,128]{2,1,0:T(1,128)S(1)}, u32[]{:S(2)}, u32[]{:S(2)}) async-start(f32[128,1,128]{2,1,0:T(1,128)} %bitcast.4), calls=%async_computation | async-start | bytes 131072 | tf_op jit(solution)/shard_map/all_to_all | solution.py:316
  33.7 11.9 %copy-start.3 = (f32[8,2048]{1,0:T(8,128)S(1)}, f32[8,2048]{1,0:T(8,128)}, u32[]{:S(2)}) copy-start(f32[8,2048]{1,0:T(8,128)} %aim_ref.1) | copy-start | bytes 196612
  33.8 11.9 %copy-start.5 = (s32[128,48]{0,1:T(8,128)S(1)}, s32[128,48]{0,1:T(8,128)}, u32[]{:S(2)}) copy-start(s32[128,48]{0,1:T(8,128)} %param.16) | copy-start | bytes 73732
  44.4 1.2 %copy-start = (f32[1024,384]{1,0:T(8,128)}, f32[1024,384]{1,0:T(8,128)S(1)}, u32[]{:S(2)}) copy-start(f32[1024,384]{1,0:T(8,128)S(1)} %shard_map.106.fields_ref) | copy-start | bytes 4718596
  45.6 29.9 %copy-start.4 = (s32[32,256]{1,0:T(8,128)S(1)}, s32[32,256]{1,0:T(8,128)}, u32[]{:S(2)}) copy-start(s32[32,256]{1,0:T(8,128)} %target_ref.1) | copy-start | bytes 98308
  56.0 19.5 %all-to-all-start.1 = ((f32[128,1,128]{2,1,0:T(1,128)}), f32[128,1,128]{2,1,0:T(1,128)S(1)}, u32[]{:S(2)}, u32[]{:S(2)}) async-start(f32[128,1,128]{2,1,0:T(1,128)} %bitcast.11), calls=%async_computation.1 | async-start | bytes 131072 | tf_op jit(solution)/shard_map/all_to_all | solution.py:350
  79.7 1.8 %collective-permute-start.4 = (f32[16,256]{1,0:T(8,128)S(1)}, f32[16,256]{1,0:T(8,128)S(1)}, u32[]{:S(2)}, u32[]{:S(2)}) collective-permute-start(f32[16,256]{1,0:T(8,128)S(1)} %get-tuple-element.30), channel_id=1, source_target_pairs={{0,16},{16,32},{32,48},{48,64},{64,80},{80,96},{96,112},{112,0},{1... | collective-permute-start | bytes 49160 | tf_op jit(solution)/shard_map/ppermute | solution.py:40
  80.7 3.5 %collective-permute-start.5 = (f32[16,256]{1,0:T(8,128)S(1)}, f32[16,256]{1,0:T(8,128)S(1)}, u32[]{:S(2)}, u32[]{:S(2)}) collective-permute-start(f32[16,256]{1,0:T(8,128)S(1)} %get-tuple-element.31), channel_id=1, source_target_pairs={{16,0},{32,16},{48,32},{64,48},{80,64},{96,80},{112,96},{0,112},{1... | collective-permute-start | bytes 49160 | tf_op jit(solution)/shard_map/ppermute | solution.py:41
  84.2 6.1 %collective-permute-start.6 = (f32[64,16]{1,0:T(8,128)S(1)}, f32[64,16]{1,0:T(8,128)S(1)}, u32[]{:S(2)}, u32[]{:S(2)}) collective-permute-start(f32[64,16]{1,0:T(8,128)S(1)} %get-tuple-element.26), channel_id=1, source_target_pairs={{0,1},{1,2},{2,3},{3,4},{4,5},{5,6},{6,7},{7,8},{8,9},{9,10},{10,1... | collective-permute-start | bytes 12296 | tf_op jit(solution)/shard_map/ppermute | solution.py:40
  84.6 5.7 %collective-permute-start.7 = (f32[64,16]{1,0:T(8,128)S(1)}, f32[64,16]{1,0:T(8,128)S(1)}, u32[]{:S(2)}, u32[]{:S(2)}) collective-permute-start(f32[64,16]{1,0:T(8,128)S(1)} %get-tuple-element.27), channel_id=1, source_target_pairs={{1,0},{2,1},{3,2},{4,3},{5,4},{6,5},{7,6},{8,7},{9,8},{10,9},{11,1... | collective-permute-start | bytes 12296 | tf_op jit(solution)/shard_map/ppermute | solution.py:41
  90.5 1.4 %copy-start.1 = (f32[1024,384]{1,0:T(8,128)S(1)}, f32[1024,384]{1,0:T(8,128)}, u32[]{:S(2)}) copy-start(f32[1024,384]{1,0:T(8,128)} %copy-done) | copy-start | bytes 4718596

commit v2 on v1

--- a/solution.py
+++ b/solution.py
@@ -13,6 +13,17 @@
 bf16 = jnp.bfloat16
 LANES = 128
 VMEM_BYTES = 48 << 20
+UNROLL = {
+    "table": 4,
+    "stack": 33,
+    "pick": 32,
+    "wide": 1,
+    "owner": 4,
+    "answer": 16,
+    "site": 4,
+    "weigh": 16,
+    "gather": 33,
+}
 
 
 def call(kernel, out_shapes, scratch=(), flops=0, moved=0, smem=(), inputs=0):
@@ -57,7 +68,7 @@
         out_ref[pl.ds(start, rows), :] = shear(line, rows).astype(bf16)
         return carry
 
-    lax.fori_loop(0, lines_ref.shape[0], one, 0)
+    lax.fori_loop(0, lines_ref.shape[0], one, 0, unroll=UNROLL["table"])
 
 
 def banded(lines, rows):
@@ -80,7 +91,7 @@
         out_ref[pl.ds(start, height), :] = moved.astype(bf16)
         return carry
 
-    lax.fori_loop(0, taps, one, 0)
+    lax.fori_loop(0, taps, one, 0, unroll=UNROLL["stack"])
     rest = out_ref.shape[0] - taps * height
     out_ref[taps * height :, :] = jnp.zeros((rest, columns), bf16)
 
@@ -114,7 +125,7 @@
             level = jnp.where(high == i * halves + half, found, level)
         return level
 
-    level = lax.fori_loop(0, rows, pick, jnp.zeros((slots, owners), f32))
+    level = lax.fori_loop(0, rows, pick, jnp.zeros((slots, owners), f32), unroll=UNROLL["pick"])
     live = lax.broadcasted_iota(jnp.int32, (slots, owners), 0) < count_ref[...]
     level = jnp.where(live, level, -1.0)
     level = jnp.concatenate([level, jnp.zeros((owners - slots, owners), f32)], axis=0)
@@ -134,7 +145,7 @@
         )
         return carry
 
-    lax.fori_loop(0, count, one, 0)
+    lax.fori_loop(0, count, one, 0, unroll=UNROLL["wide"])
 
 
 def split(x):
@@ -151,43 +162,53 @@
     return lax.dot_general(a, b, (((1,), (1,)), ((), ())), preferred_element_type=f32)
 
 
-def owner_kernel(dose_ref, level_ref, frag_ref, aim_ref, error_ref, slope_ref, level_t, slope_t):
+def side_by_side(ref):
+    return jnp.concatenate([ref[c] for c in range(ref.shape[0])], axis=1)
+
+
+def owner_kernel(
+    dose_ref,
+    level_ref,
+    frag_ref,
+    aim_ref,
+    error_ref,
+    slope_ref,
+    level_t,
+    slope_t,
+    resist_ref,
+    value_ref,
+    place_ref,
+):
     slots = frag_ref.shape[0]
     conds = dose_ref.shape[0]
     bins = aim_ref.shape[1] // LANES
     level_t[...] = level_ref[...].T
     dose = jnp.broadcast_to(dose_ref[...], (conds, LANES))
 
-    def resist_of(c):
+    def place(c, carry):
         level = jnp.broadcast_to(level_t[pl.ds(c, 1), :], (conds, LANES))
-        return level, jax.nn.sigmoid(steepness * (dose * level - threshold))
-
-    def add(pair, total):
-        left, right = [], []
-        for c in (2 * pair, 2 * pair + 1):
-            level, resist = resist_of(c)
-            frag = jnp.broadcast_to(frag_ref[pl.ds(c, 1), :], (conds, LANES))
-            top, rest = split(jnp.where(level >= 0.0, resist, 0.0))
-            bin_of = frag >> 7
-            left.append(
-                jnp.concatenate(
-                    [jnp.where(bin_of == q, part, 0.0) for part in (top, rest) for q in range(bins)],
-                    axis=0,
-                ).astype(bf16)
-            )
-            right.append(one_hot(frag_ref[pl.ds(c, 1), :] & (LANES - 1), LANES))
-        return total + product_nt(
-            jnp.concatenate(left, axis=1), jnp.concatenate(right, axis=1)
-        )
-
-    total = lax.fori_loop(0, slots // 2, add, jnp.zeros((2 * bins * conds, LANES), f32))
+        resist = jax.nn.sigmoid(steepness * (dose * level - threshold))
+        live = level >= 0.0
+        resist_ref[c] = jnp.where(live, resist, 0.0)
+        top, rest = split(jnp.where(live, resist, 0.0))
+        frag = frag_ref[pl.ds(c, 1), :]
+        bin_of = jnp.broadcast_to(frag >> 7, (conds, LANES))
+        value_ref[c] = jnp.concatenate(
+            [jnp.where(bin_of == q, part, 0.0) for part in (top, rest) for q in range(bins)],
+            axis=0,
+        ).astype(bf16)
+        place_ref[c] = one_hot(frag & (LANES - 1), LANES)
+        return carry
+
+    lax.fori_loop(0, slots, place, 0, unroll=UNROLL["owner"])
+    total = product_nt(side_by_side(value_ref), side_by_side(place_ref))
     total = total[: bins * conds] + total[bins * conds :]
     for q in range(bins):
         lanes = slice(q * LANES, (q + 1) * LANES)
         error_ref[:, lanes] = total[q * conds : (q + 1) * conds] - aim_ref[:, lanes]
 
     def answer(c, carry):
-        level, resist = resist_of(c)
+        resist = resist_ref[c]
         frag = jnp.broadcast_to(frag_ref[pl.ds(c, 1), :], (conds, LANES))
         low = frag & (LANES - 1)
         bin_of = frag >> 7
@@ -198,42 +219,37 @@
             )
             reply = jnp.where(bin_of == q, found, reply)
         terms = reply * steepness * dose * resist * (1.0 - resist)
-        terms = jnp.where(level >= 0.0, terms, 0.0)
         slope_t[pl.ds(c, 1), :] = jnp.sum(terms, axis=0, keepdims=True)
         return carry
 
-    lax.fori_loop(0, slots, answer, 0)
+    lax.fori_loop(0, slots, answer, 0, unroll=UNROLL["answer"])
     slope_t[slots:, :] = jnp.zeros((LANES - slots, LANES), f32)
     slope_ref[...] = slope_t[...].T
 
 
-def site_kernel(reply_ref, pix_ref, inten_ref, target_ref, slope_ref, reply_t):
+def site_kernel(
+    reply_ref, pix_ref, inten_ref, target_ref, slope_ref, reply_t, value_ref, place_ref
+):
     rows, columns = inten_ref.shape
     slots = pix_ref.shape[0]
     halves = columns // LANES
+    size = rows * halves
     reply_t[...] = reply_ref[...].T
 
-    def add(pair, total):
-        left, right = [], []
-        for c in (2 * pair, 2 * pair + 1):
-            pix = pix_ref[pl.ds(c, 1), :]
-            line = pix >> 7
-            line = (line % halves) * rows + line // halves
-            ids = lax.broadcasted_iota(jnp.int32, (rows * halves, LANES), 0)
-            top, rest = split(reply_t[pl.ds(c, 1), :])
-            here = ids == line
-            left.append(
-                jnp.concatenate(
-                    [jnp.where(here, top, 0.0), jnp.where(here, rest, 0.0)], axis=0
-                ).astype(bf16)
-            )
-            right.append(one_hot(pix & (LANES - 1), LANES))
-        return total + product_nt(
-            jnp.concatenate(left, axis=1), jnp.concatenate(right, axis=1)
-        )
-
-    size = rows * halves
-    total = lax.fori_loop(0, slots // 2, add, jnp.zeros((2 * size, LANES), f32))
+    def place(c, carry):
+        pix = pix_ref[pl.ds(c, 1), :]
+        line = pix >> 7
+        line = (line % halves) * rows + line // halves
+        here = lax.broadcasted_iota(jnp.int32, (size, LANES), 0) == line
+        top, rest = split(reply_t[pl.ds(c, 1), :])
+        value_ref[c] = jnp.concatenate(
+            [jnp.where(here, top, 0.0), jnp.where(here, rest, 0.0)], axis=0
+        ).astype(bf16)
+        place_ref[c] = one_hot(pix & (LANES - 1), LANES)
+        return carry
+
+    lax.fori_loop(0, slots, place, 0, unroll=UNROLL["site"])
+    total = product_nt(side_by_side(value_ref), side_by_side(place_ref))
     total = total[:size] + total[size:]
     for half in range(halves):
         lanes = slice(half * LANES, (half + 1) * LANES)
@@ -254,14 +270,14 @@
         weighted_ref[pl.ds(start, height), :] = (gain_ref[h // 2] * field * slope).astype(bf16)
         return carry
 
-    lax.fori_loop(0, weighted_ref.shape[0] // height, weigh, 0)
+    lax.fori_loop(0, weighted_ref.shape[0] // height, weigh, 0, unroll=UNROLL["weigh"])
     part_ref[...] = jnp.dot(table_ref[...], weighted_ref[...], preferred_element_type=f32)
 
     def gather(v, total):
         start = pl.multiple_of(v * rows, rows)
         return total + pltpu.roll(part_ref[pl.ds(start, rows), :], width - v, axis=1)[:, :columns]
 
-    total = lax.fori_loop(0, taps, gather, jnp.zeros((rows, columns), f32))
+    total = lax.fori_loop(0, taps, gather, jnp.zeros((rows, columns), f32), unroll=UNROLL["gather"])
     out_ref[...] = 2.0 * total
 
 
@@ -282,7 +298,8 @@
     reach = extent // 2
     kernel_taps = kernels.reshape(-1, extent, extent)
     parts = kernel_taps.shape[0]
-    owners = site_pix.shape[0]
+    owners, slots = site_pix.shape
+    conds = doses.shape[0]
     both = ("row", "col")
 
     near = ring_halo(mask, "row", 0, 2 * reach)
@@ -318,7 +335,7 @@
     tall = rows + 4 * reach
     wide_depth = round_up(extent * tall, LANES)
     wide_fields = call(
-        functools.partial(wide_kernel, extent, height, 256),
+        functools.partial(wide_kernel, extent, height, 512),
         jax.ShapeDtypeStruct((parts * height, wide_columns), f32),
         scratch=[
             pltpu.VMEM((parts * height, wide_depth), bf16),
@@ -337,7 +354,13 @@
             jax.ShapeDtypeStruct(frag_target.shape, f32),
             jax.ShapeDtypeStruct((owners, LANES), f32),
         ),
-        scratch=[pltpu.VMEM((LANES, LANES), f32)] * 2,
+        scratch=[
+            pltpu.VMEM((LANES, LANES), f32),
+            pltpu.VMEM((LANES, LANES), f32),
+            pltpu.VMEM((slots, conds, LANES), f32),
+            pltpu.VMEM((slots, 2 * frag_target.size // LANES, LANES), bf16),
+            pltpu.VMEM((slots, LANES, LANES), bf16),
+        ],
         inputs=4,
         flops=2 * 2 * frag_target.size * site_pix.size // 16,
         moved=8 * frag_target.size,
@@ -353,7 +376,11 @@
     slope = call(
         site_kernel,
         jax.ShapeDtypeStruct((rows, columns), f32),
-        scratch=[pltpu.VMEM((LANES, LANES), f32)],
+        scratch=[
+            pltpu.VMEM((LANES, LANES), f32),
+            pltpu.VMEM((slots, 2 * rows * columns // LANES, LANES), bf16),
+            pltpu.VMEM((slots, LANES, LANES), bf16),
+        ],
         inputs=4,
         flops=2 * 2 * rows * columns * site_pix.size // 64,
         moved=16 * rows * columns,

time: 98.2 us -> 76.2 us (0.78)
  Pallas kernels: 43.8 us -> 20 us
  waiting for transfers between devices: 13.6 us -> 17.5 us
  starting transfers between devices: 33.8 us -> 31.7 us
    pallas_call x1, Pallas kernels: 10.3 us -> 3.93 us  [body(): call(owner_kernel, (jax.ShapeDtypeStruct(frag_target.shape, f32), jax.Sha...]
    pallas_call x1, Pallas kernels: 8.22 us -> 3.46 us  [body(): call(functools.partial(forward_kernel, extent, reach), (jax.ShapeDtypeStr...]
    pallas_call x1, Pallas kernels: 10.7 us -> 6.43 us  [body(): call(functools.partial(wide_kernel, extent, height, 512), jax.ShapeDtypeS...]
    pallas_call x1, Pallas kernels: 5.61 us -> 2.71 us  [body(): call(functools.partial(back_kernel, extent), jax.ShapeDtypeStruct((rows,...]
    pallas_call x2, Pallas kernels: 4.85 us -> 2.09 us  [banded(): call(functools.partial(table_kernel, rows), jax.ShapeDtypeStruct((count *...]
    pallas_call x1, Pallas kernels: 4.16 us -> 1.41 us  [body(): call(site_kernel, jax.ShapeDtypeStruct((rows, columns), f32), scratch=[pl...]
    all_to_all x1, waiting for transfers between devices: 0.01 us -> 2.06 us  [body(): lax.all_to_all(level, both, split_axis=0, concat_axis=0, tiled=True)]
    all_to_all x1, starting transfers between devices: 9.76 us -> 7.71 us  [body(): lax.all_to_all(answers, both, split_axis=0, concat_axis=0, tiled=True)]
  transfers between devices with their start and end apart: 10 -> 10, of which waited for: 6 -> 7; matrix products, arithmetic and copies ran while one was open for 2% -> 3% of each run, Pallas kernels for 16% -> 11%
where the time goes in v2:
time: 76.2 us; the launch traced here: 75.5 us
  starting transfers between devices  31.7 us (42%)
  Pallas kernels  20 us (26%)
  waiting for transfers between devices  17.5 us (23%)
  local copies, waits for them, and re-layouts  5.01 us (7%)
  between operations  0.92 us (1%)
    ppermute x4, starting transfers between devices, ring_halo(): high = lax.ppermute(lax.slice_in_dim(block, 0, width, axis=dim), axis, down)  9.44 us
    all_to_all x1, starting transfers between devices, body(): lax.all_to_all(level, both, split_axis=0, concat_axis=0, tiled=True)  9.31 us
    all_to_all x1, waiting for transfers between devices, body(): lax.all_to_all(answers, both, split_axis=0, concat_axis=0, tiled=True)  8.54 us
    all_to_all x1, starting transfers between devices, body(): lax.all_to_all(answers, both, split_axis=0, concat_axis=0, tiled=True)  7.71 us
    pallas_call x1, Pallas kernels, body(): call(functools.partial(wide_kernel, extent, height, 512), jax.ShapeDtypeS...  6.43 us
    ppermute x4, starting transfers between devices, ring_halo(): lax.ppermute(lax.slice_in_dim(block, size - width, size, axis=dim), axis,...  5.27 us
    ppermute x4, waiting for transfers between devices, ring_halo(): high = lax.ppermute(lax.slice_in_dim(block, 0, width, axis=dim), axis, down)  4.72 us
    pallas_call x1, Pallas kernels, body(): call(owner_kernel, (jax.ShapeDtypeStruct(frag_target.shape, f32), jax.Sha...  3.93 us
  transfers between devices with their start and end apart: 10, of which 7 were waited for; matrix products, arithmetic and copies ran while one was open for 3% of the time, Pallas kernels for 11%

profile of v2, /device:TPU:1, one launch (start us, length us, event | category | flops | bytes accessed | tf_op | source)
XLA Modules:
  0.0 75.5 jit_solution(8134263144479275053)
XLA Ops:
  0.6 2.6 %collective-permute-start = (bf16[32,256]{1,0:T(8,128)(2,1)}, bf16[32,256]{1,0:T(8,128)(2,1)S(1)}, u32[]{:S(2)}, u32[]{:S(2)}) collective-permute-start(bf16[32,256]{1,0:T(8,128)(2,1)} %param.9), channel_id=1, source_target_pairs={{0,16},{16,32},{32,48},{48,64},{64,80},{80,96},{96,112},{112,0},{1... | collective-permute-start | bytes 49160 | tf_op jit(solution)/shard_map/ppermute | solution.py:51
  3.3 1.0 %copy.26 = bf16[8,2,33,33]{3,1,0,2:T(2,128)(2,1)S(1)} copy(bf16[8,2,33,33]{3,1,2,0:T(2,128)(2,1)} %param.11) | data formatting | bytes 69696 | tf_op args[2]
  5.4 1.2 %collective-permute-done.1 = bf16[32,256]{1,0:T(8,128)(2,1)S(1)} collective-permute-done((bf16[32,256]{1,0:T(8,128)(2,1)}, bf16[32,256]{1,0:T(8,128)(2,1)S(1)}, u32[]{:S(2)}, u32[]{:S(2)}) %collective-permute-start.1) | collective-permute-done | bytes 16416 | tf_op jit(solution)/shard_map/ppermute | solution.py:52
  6.7 1.3 %collective-permute-start.2 = (bf16[96,32]{1,0:T(8,128)(2,1)S(1)}, bf16[96,32]{1,0:T(8,128)(2,1)S(1)}, u32[]{:S(2)}, u32[]{:S(2)}) collective-permute-start(bf16[96,32]{1,0:T(8,128)(2,1)S(1)} %get-tuple-element.28), channel_id=1, source_target_pairs={{0,1},{1,2},{2,3},{3,4},{4,5},{5,6},{6,7},{7,8},{8,9},{9,10},{10,1... | collective-permute-start | bytes 18440 | tf_op jit(solution)/shard_map/ppermute | solution.py:51
  8.3 0.9 %shard_map.104.table_ref = bf16[512,2176]{1,0:T(8,128)(2,1)S(1)} custom-call(f32[16,2176]{1,0:T(8,128)S(1)} %pad_convert_fusion.2.lines_ref), custom_call_target="tpu_custom_call" | custom-call | bytes 2228224 | tf_op jit(solution)/shard_map/pallas_call | solution.py:76
  9.2 5.0 %collective-permute-start.3 = (bf16[96,32]{1,0:T(8,128)(2,1)S(1)}, bf16[96,32]{1,0:T(8,128)(2,1)S(1)}, u32[]{:S(2)}, u32[]{:S(2)}) collective-permute-start(bf16[96,32]{1,0:T(8,128)(2,1)S(1)} %get-tuple-element.29), channel_id=1, source_target_pairs={{1,0},{2,1},{3,2},{4,3},{5,4},{6,5},{7,6},{8,7},{9,8},{10,9},{11,1... | collective-permute-start | bytes 18440 | tf_op jit(solution)/shard_map/ppermute | solution.py:52
  14.2 0.9 %collective-permute-done.3 = bf16[96,32]{1,0:T(8,128)(2,1)S(1)} collective-permute-done((bf16[96,32]{1,0:T(8,128)(2,1)S(1)}, bf16[96,32]{1,0:T(8,128)(2,1)S(1)}, u32[]{:S(2)}, u32[]{:S(2)}) %collective-permute-start.3) | collective-permute-done | bytes 6176 | tf_op jit(solution)/shard_map/ppermute | solution.py:52
  15.3 3.5 %shard_map.105 = (f32[128,128]{1,0:T(8,128)}, f32[32,256]{1,0:T(8,128)S(1)}) custom-call(f32[8]{0:T(128)S(1)} %copy-done.6, bf16[96,384]{1,0:T(8,128)(2,1)S(1)} %fusion.11.mask_ref, bf16[512,2176]{1,0:T(8,128)(2,1)S(1)} %shard_map.104.table_ref, s32[48,128]{1,0:T(8,128)S(1)} %bitcast.17, s32[1,128]{1,0:T(1,128)S(1)} %copy-done.7), custom_call_target="tpu_custom_call" | custom-call | flops 570425344 | bytes 2228224 | tf_op jit(solution)/shard_map/pallas_call | solution.py:316
  18.7 9.3 %all-to-all-start = ((f32[128,1,128]{2,1,0:T(1,128)}), f32[128,1,128]{2,1,0:T(1,128)S(1)}, u32[]{:S(2)}, u32[]{:S(2)}) async-start(f32[128,1,128]{2,1,0:T(1,128)} %bitcast.4), calls=%async_computation | async-start | bytes 131072 | tf_op jit(solution)/shard_map/all_to_all | solution.py:333
  28.1 6.4 %shard_map.106.fields_ref = f32[1024,384]{1,0:T(8,128)S(1)} custom-call(bf16[96,384]{1,0:T(8,128)(2,1)S(1)} %fusion.11.mask_ref, f32[16,3200]{1,0:T(8,128)S(1)} %pad_convert_fusion.1.lines_ref), custom_call_target="tpu_custom_call" | custom-call | flops 2516582400 | bytes 1572864 | tf_op jit(solution)/shard_map/pallas_call | solution.py:337
  34.5 1.2 %copy-done = f32[1024,384]{1,0:T(8,128)} copy-done((f32[1024,384]{1,0:T(8,128)}, f32[1024,384]{1,0:T(8,128)S(1)}, u32[]{:S(2)}) %copy-start) | copy-done | bytes 1572888
  35.7 2.1 %all-to-all-done = f32[128,1,128]{2,1,0:T(1,128)S(1)} async-done(((f32[128,1,128]{2,1,0:T(1,128)}), f32[128,1,128]{2,1,0:T(1,128)S(1)}, u32[]{:S(2)}, u32[]{:S(2)}) %all-to-all-start) | async-done | bytes 65568 | tf_op jit(solution)/shard_map/all_to_all | solution.py:333
  37.7 3.9 %shard_map.107 = (f32[8,2048]{1,0:T(8,128)}, f32[128,128]{1,0:T(8,128)}) custom-call(f32[8,1]{1,0:T(8,128)S(1)} %copy.30.dose_ref, f32[128,128]{1,0:T(8,128)S(1)} %bitcast.16, s32[48,128]{1,0:T(8,128)S(1)} %bitcast.19, f32[8,2048]{1,0:T(8,128)S(1)} %copy-done.3), custom_call_target="tpu_custom_call" | custom-call | flops 25165824 | bytes 131072 | tf_op jit(solution)/shard_map/pallas_call | solution.py:351
  41.7 7.7 %all-to-all-start.1 = ((f32[128,1,128]{2,1,0:T(1,128)}), f32[128,1,128]{2,1,0:T(1,128)S(1)}, u32[]{:S(2)}, u32[]{:S(2)}) async-start(f32[128,1,128]{2,1,0:T(1,128)} %bitcast.11), calls=%async_computation.1 | async-start | bytes 131072 | tf_op jit(solution)/shard_map/all_to_all | solution.py:373
  49.4 1.2 %shard_map.108.table_ref = bf16[1056,1024]{1,0:T(8,128)(2,1)S(1)} custom-call(f32[33,1024]{1,0:T(8,128)S(1)} %reshape.23.lines_ref), custom_call_target="tpu_custom_call" | custom-call | bytes 2162688 | tf_op jit(solution)/shard_map/pallas_call | solution.py:76
  50.6 8.5 %all-to-all-done.1 = f32[128,1,128]{2,1,0:T(1,128)S(1)} async-done(((f32[128,1,128]{2,1,0:T(1,128)}), f32[128,1,128]{2,1,0:T(1,128)S(1)}, u32[]{:S(2)}, u32[]{:S(2)}) %all-to-all-start.1) | async-done | bytes 65568 | tf_op jit(solution)/shard_map/all_to_all | solution.py:373
  59.2 1.4 %shard_map.109 = f32[32,256]{1,0:T(8,128)S(1)} custom-call(f32[128,128]{1,0:T(8,128)S(1)} %bitcast.15, s32[48,128]{1,0:T(8,128)S(1)} %bitcast.18, f32[32,256]{1,0:T(8,128)S(1)} %get-tuple-element.23.inten_ref, s32[32,256]{1,0:T(8,128)S(1)} %copy-done.4), custom_call_target="tpu_custom_call" | custom-call | flops 3145728 | bytes 131072 | tf_op jit(solution)/shard_map/pallas_call | solution.py:376
  60.6 1.0 %collective-permute-start.4 = (f32[16,256]{1,0:T(8,128)S(1)}, f32[16,256]{1,0:T(8,128)S(1)}, u32[]{:S(2)}, u32[]{:S(2)}) collective-permute-start(f32[16,256]{1,0:T(8,128)S(1)} %get-tuple-element.30), channel_id=1, source_target_pairs={{0,16},{16,32},{32,48},{48,64},{64,80},{80,96},{96,112},{112,0},{1... | collective-permute-start | bytes 49160 | tf_op jit(solution)/shard_map/ppermute | solution.py:51
  61.6 0.9 %collective-permute-done.4 = f32[16,256]{1,0:T(8,128)S(1)} collective-permute-done((f32[16,256]{1,0:T(8,128)S(1)}, f32[16,256]{1,0:T(8,128)S(1)}, u32[]{:S(2)}, u32[]{:S(2)}) %collective-permute-start.4) | collective-permute-done | bytes 16416 | tf_op jit(solution)/shard_map/ppermute | solution.py:51
  62.5 2.6 %collective-permute-done.5 = f32[16,256]{1,0:T(8,128)S(1)} collective-permute-done((f32[16,256]{1,0:T(8,128)S(1)}, f32[16,256]{1,0:T(8,128)S(1)}, u32[]{:S(2)}, u32[]{:S(2)}) %collective-permute-start.5) | collective-permute-done | bytes 16416 | tf_op jit(solution)/shard_map/ppermute | solution.py:52
  65.5 4.4 %collective-permute-start.7 = (f32[64,16]{1,0:T(8,128)S(1)}, f32[64,16]{1,0:T(8,128)S(1)}, u32[]{:S(2)}, u32[]{:S(2)}) collective-permute-start(f32[64,16]{1,0:T(8,128)S(1)} %get-tuple-element.27), channel_id=1, source_target_pairs={{1,0},{2,1},{3,2},{4,3},{5,4},{6,5},{7,6},{8,7},{9,8},{10,9},{11,1... | collective-permute-start | bytes 12296 | tf_op jit(solution)/shard_map/ppermute | solution.py:52
  69.9 1.3 %collective-permute-done.6 = f32[64,16]{1,0:T(8,128)S(1)} collective-permute-done((f32[64,16]{1,0:T(8,128)S(1)}, f32[64,16]{1,0:T(8,128)S(1)}, u32[]{:S(2)}, u32[]{:S(2)}) %collective-permute-start.6) | collective-permute-done | bytes 4128 | tf_op jit(solution)/shard_map/ppermute | solution.py:51
  71.4 1.4 %copy-done.1 = f32[1024,384]{1,0:T(8,128)S(1)} copy-done((f32[1024,384]{1,0:T(8,128)S(1)}, f32[1024,384]{1,0:T(8,128)}, u32[]{:S(2)}) %copy-start.1) | copy-done | bytes 1572888
  72.8 2.7 %shard_map.110 = f32[32,256]{1,0:T(8,128)} custom-call(f32[8]{0:T(128)S(1)} %copy-done.6, f32[1024,384]{1,0:T(8,128)S(1)} %copy-done.1, f32[64,384]{1,0:T(8,128)S(1)} %select_maximum_fusion.slope_ref, bf16[1056,1024]{1,0:T(8,128)(2,1)S(1)} %shard_map.108.table_ref), custom_call_target="tpu_custom_call" | custom-call | flops 830472192 | bytes 3145728 | tf_op jit(solution)/shard_map/pallas_call | solution.py:392
  (51 shorter events, 2.1 us)
Async XLA Ops:
  0.6 6.0 %copy-start.8 = (bf16[32,256]{1,0:T(8,128)(2,1)S(1)}, bf16[32,256]{1,0:T(8,128)(2,1)}, u32[]{:S(2)}) copy-start(bf16[32,256]{1,0:T(8,128)(2,1)} %param.9) | copy-start | bytes 49156
  0.6 7.4 %copy-start.9 = (f32[8]{0:T(128)S(1)}, f32[8]{0:T(128)}, u32[]{:S(2)}) copy-start(f32[8]{0:T(128)} %param.13) | copy-start | bytes 100
  0.6 4.8 %collective-permute-start = (bf16[32,256]{1,0:T(8,128)(2,1)}, bf16[32,256]{1,0:T(8,128)(2,1)S(1)}, u32[]{:S(2)}, u32[]{:S(2)}) collective-permute-start(bf16[32,256]{1,0:T(8,128)(2,1)} %param.9), channel_id=1, source_target_pairs={{0,16},{16,32},{32,48},{48,64},{64,80},{80,96},{96,112},{112,0},{1... | collective-permute-start | bytes 49160 | tf_op jit(solution)/shard_map/ppermute | solution.py:51
  3.3 3.4 %collective-permute-start.1 = (bf16[32,256]{1,0:T(8,128)(2,1)}, bf16[32,256]{1,0:T(8,128)(2,1)S(1)}, u32[]{:S(2)}, u32[]{:S(2)}) collective-permute-start(bf16[32,256]{1,0:T(8,128)(2,1)} %param.9), channel_id=1, source_target_pairs={{16,0},{32,16},{48,32},{64,48},{80,64},{96,80},{112,96},{0,112},{1... | collective-permute-start | bytes 49160 | tf_op jit(solution)/shard_map/ppermute | solution.py:52
  5.0 10.3 %copy-start.2 = (s32[128,48]{0,1:T(8,128)S(1)}, s32[128,48]{0,1:T(8,128)}, u32[]{:S(2)}) copy-start(s32[128,48]{0,1:T(8,128)} %param.14) | copy-start | bytes 73732
  5.0 10.3 %copy-start.6 = (f32[8]{0:T(128)S(1)}, f32[8]{0:T(128)}, u32[]{:S(2)}) copy-start(f32[8]{0:T(128)} %gain_ref.3) | copy-start | bytes 100
  5.0 10.3 %copy-start.7 = (s32[1,128]{1,0:T(1,128)S(1)}, s32[1,128]{1,0:T(1,128)}, u32[]{:S(2)}) copy-start(s32[1,128]{1,0:T(1,128)} %count_ref.1) | copy-start | bytes 1540
  6.7 7.4 %collective-permute-start.2 = (bf16[96,32]{1,0:T(8,128)(2,1)S(1)}, bf16[96,32]{1,0:T(8,128)(2,1)S(1)}, u32[]{:S(2)}, u32[]{:S(2)}) collective-permute-start(bf16[96,32]{1,0:T(8,128)(2,1)S(1)} %get-tuple-element.28), channel_id=1, source_target_pairs={{0,1},{1,2},{2,3},{3,4},{4,5},{5,6},{6,7},{7,8},{8,9},{9,10},{10,1... | collective-permute-start | bytes 18440 | tf_op jit(solution)/shard_map/ppermute | solution.py:51
  9.2 5.9 %collective-permute-start.3 = (bf16[96,32]{1,0:T(8,128)(2,1)S(1)}, bf16[96,32]{1,0:T(8,128)(2,1)S(1)}, u32[]{:S(2)}, u32[]{:S(2)}) collective-permute-start(bf16[96,32]{1,0:T(8,128)(2,1)S(1)} %get-tuple-element.29), channel_id=1, source_target_pairs={{1,0},{2,1},{3,2},{4,3},{5,4},{6,5},{7,6},{8,7},{9,8},{10,9},{11,1... | collective-permute-start | bytes 18440 | tf_op jit(solution)/shard_map/ppermute | solution.py:52
  18.7 19.0 %all-to-all-start = ((f32[128,1,128]{2,1,0:T(1,128)}), f32[128,1,128]{2,1,0:T(1,128)S(1)}, u32[]{:S(2)}, u32[]{:S(2)}) async-start(f32[128,1,128]{2,1,0:T(1,128)} %bitcast.4), calls=%async_computation | async-start | bytes 131072 | tf_op jit(solution)/shard_map/all_to_all | solution.py:333
  28.0 9.7 %copy-start.3 = (f32[8,2048]{1,0:T(8,128)S(1)}, f32[8,2048]{1,0:T(8,128)}, u32[]{:S(2)}) copy-start(f32[8,2048]{1,0:T(8,128)} %aim_ref.1) | copy-start | bytes 196612
  28.0 9.7 %copy-start.5 = (s32[128,48]{0,1:T(8,128)S(1)}, s32[128,48]{0,1:T(8,128)}, u32[]{:S(2)}) copy-start(s32[128,48]{0,1:T(8,128)} %param.16) | copy-start | bytes 73732
  34.5 1.2 %copy-start = (f32[1024,384]{1,0:T(8,128)}, f32[1024,384]{1,0:T(8,128)S(1)}, u32[]{:S(2)}) copy-start(f32[1024,384]{1,0:T(8,128)S(1)} %shard_map.106.fields_ref) | copy-start | bytes 4718596
  35.7 23.5 %copy-start.4 = (s32[32,256]{1,0:T(8,128)S(1)}, s32[32,256]{1,0:T(8,128)}, u32[]{:S(2)}) copy-start(s32[32,256]{1,0:T(8,128)} %target_ref.1) | copy-start | bytes 98308
  41.7 17.5 %all-to-all-start.1 = ((f32[128,1,128]{2,1,0:T(1,128)}), f32[128,1,128]{2,1,0:T(1,128)S(1)}, u32[]{:S(2)}, u32[]{:S(2)}) async-start(f32[128,1,128]{2,1,0:T(1,128)} %bitcast.11), calls=%async_computation.1 | async-start | bytes 131072 | tf_op jit(solution)/shard_map/all_to_all | solution.py:373
  60.6 1.9 %collective-permute-start.4 = (f32[16,256]{1,0:T(8,128)S(1)}, f32[16,256]{1,0:T(8,128)S(1)}, u32[]{:S(2)}, u32[]{:S(2)}) collective-permute-start(f32[16,256]{1,0:T(8,128)S(1)} %get-tuple-element.30), channel_id=1, source_target_pairs={{0,16},{16,32},{32,48},{48,64},{64,80},{80,96},{96,112},{112,0},{1... | collective-permute-start | bytes 49160 | tf_op jit(solution)/shard_map/ppermute | solution.py:51
  61.6 3.5 %collective-permute-start.5 = (f32[16,256]{1,0:T(8,128)S(1)}, f32[16,256]{1,0:T(8,128)S(1)}, u32[]{:S(2)}, u32[]{:S(2)}) collective-permute-start(f32[16,256]{1,0:T(8,128)S(1)} %get-tuple-element.31), channel_id=1, source_target_pairs={{16,0},{32,16},{48,32},{64,48},{80,64},{96,80},{112,96},{0,112},{1... | collective-permute-start | bytes 49160 | tf_op jit(solution)/shard_map/ppermute | solution.py:52
  65.1 6.1 %collective-permute-start.6 = (f32[64,16]{1,0:T(8,128)S(1)}, f32[64,16]{1,0:T(8,128)S(1)}, u32[]{:S(2)}, u32[]{:S(2)}) collective-permute-start(f32[64,16]{1,0:T(8,128)S(1)} %get-tuple-element.26), channel_id=1, source_target_pairs={{0,1},{1,2},{2,3},{3,4},{4,5},{5,6},{6,7},{7,8},{8,9},{9,10},{10,1... | collective-permute-start | bytes 12296 | tf_op jit(solution)/shard_map/ppermute | solution.py:51
  65.5 5.7 %collective-permute-start.7 = (f32[64,16]{1,0:T(8,128)S(1)}, f32[64,16]{1,0:T(8,128)S(1)}, u32[]{:S(2)}, u32[]{:S(2)}) collective-permute-start(f32[64,16]{1,0:T(8,128)S(1)} %get-tuple-element.27), channel_id=1, source_target_pairs={{1,0},{2,1},{3,2},{4,3},{5,4},{6,5},{7,6},{8,7},{9,8},{10,9},{11,1... | collective-permute-start | bytes 12296 | tf_op jit(solution)/shard_map/ppermute | solution.py:52
  71.4 1.4 %copy-start.1 = (f32[1024,384]{1,0:T(8,128)S(1)}, f32[1024,384]{1,0:T(8,128)}, u32[]{:S(2)}) copy-start(f32[1024,384]{1,0:T(8,128)} %copy-done) | copy-start | bytes 4718596

commit v3 on v2

v3 whole, which is shorter than its diff:
```python
import functools

import jax
import jax.numpy as jnp
from jax import lax
from jax.experimental import pallas as pl
from jax.experimental.pallas import tpu as pltpu
from jax.sharding import PartitionSpec as P

steepness = 4.0
threshold = 1.2
f32 = jnp.float32
bf16 = jnp.bfloat16
LANES = 128
NEIGHBOURS = [(down, right) for right in (-1, 0, 1) for down in (-1, 0, 1)]
MIB = 1 << 20
UNROLL = {
    "table": 4,
    "stack": 33,
    "pick": 32,
    "owner": 4,
    "answer": 16,
    "site": 4,
    "weigh": 16,
    "gather": 33,
}


def call(
    kernel, out_shapes, scratch=(), flops=0, moved=0, smem=(), hbm=(), hbm_out=(), inputs=0, vmem_mib=16
):
    vmem = pl.BlockSpec(memory_space=pltpu.VMEM)
    specs = [vmem] * inputs
    for i in smem:
        specs[i] = pl.BlockSpec(memory_space=pltpu.SMEM)
    for i in hbm:
        specs[i] = pl.BlockSpec(memory_space=pltpu.HBM)
    out_specs = jax.tree.map(lambda _: vmem, out_shapes)
    if hbm_out:
        out_specs = tuple(
            pl.BlockSpec(memory_space=pltpu.HBM) if i in hbm_out else vmem
            for i in range(len(out_shapes))
        )
    return pl.pallas_call(
        kernel,
        out_shape=out_shapes,
        in_specs=specs,
        out_specs=out_specs,
        scratch_shapes=list(scratch),
        cost_estimate=pl.CostEstimate(flops=flops, bytes_accessed=moved, transcendentals=0),
        compiler_params=pltpu.CompilerParams(vmem_limit_bytes=vmem_mib * MIB),
    )


def ring(low_end, high_end, axis):
    count = lax.axis_size(axis)
    up = [(i, (i + 1) % count) for i in range(count)]
    down = [(target, source) for source, target in up]
    return lax.ppermute(high_end, axis, up), lax.ppermute(low_end, axis, down)


def clipped(low, high, axis):
    index = lax.axis_index(axis)
    zero = jnp.zeros((), low.dtype)
    low = jnp.where(index == 0, zero, low)
    return low, jnp.where(index == lax.axis_size(axis) - 1, zero, high)


def shear(row, rows):
    wide = jnp.broadcast_to(row, (rows, row.shape[1]))
    return pltpu.roll(wide, 0, axis=1, stride=1, stride_axis=0)


def table_kernel(rows, lines_ref, out_ref):
    def one(index, carry):
        line = lines_ref[pl.ds(index, 1), :]
        start = pl.multiple_of(index * rows, rows)
        out_ref[pl.ds(start, rows), :] = shear(line, rows).astype(bf16)
        return carry

    lax.fori_loop(0, lines_ref.shape[0], one, 0, unroll=UNROLL["table"])


def banded(lines, rows, hbm=False):
    count, width = lines.shape
    return call(
        functools.partial(table_kernel, rows),
        jax.ShapeDtypeStruct((count * rows, width), bf16),
        inputs=1,
        moved=2 * count * rows * width,
    )(lines)


def stack_shifts(plane, taps, first, out_ref):
    height, width = plane.shape
    columns = out_ref.shape[1]

    def one(v, carry):
        moved = pltpu.roll(plane, width - first - v, axis=1)[:, :columns]
        start = pl.multiple_of(v * height, height)
        out_ref[pl.ds(start, height), :] = moved.astype(bf16)
        return carry

    lax.fori_loop(0, taps, one, 0, unroll=UNROLL["stack"])
    rest = out_ref.shape[0] - taps * height
    out_ref[taps * height :, :] = jnp.zeros((rest, columns), bf16)


def forward_kernel(
    taps, reach, gain_ref, mask_ref, table_ref, pix_ref, count_ref, level_ref, stack_ref, lines_ref
):
    columns = stack_ref.shape[1]
    halves = columns // LANES
    rows = lines_ref.shape[0] // halves
    plane = mask_ref[reach : reach + rows + 2 * reach, :].astype(f32)
    stack_shifts(plane, taps, reach, stack_ref)
    fields = jnp.dot(table_ref[...], stack_ref[...], preferred_element_type=f32)
    total = jnp.zeros((rows, columns), f32)
    for k in range(gain_ref.shape[0]):
        real = fields[2 * k * rows : (2 * k + 1) * rows]
        imag = fields[(2 * k + 1) * rows : (2 * k + 2) * rows]
        total = total + gain_ref[k] * (real * real + imag * imag)
    for half in range(halves):
        lines_ref[half * rows : (half + 1) * rows, :] = total[:, half * LANES : (half + 1) * LANES]
    pix = pix_ref[...]
    slots, owners = pix.shape
    low = pix & (LANES - 1)
    high = pix >> 7

    def pick(i, level):
        for half in range(halves):
            line = lines_ref[pl.ds(half * rows + i, 1), :]
            wide = jnp.broadcast_to(line, (slots, LANES))
            found = jnp.take_along_axis(wide, low, axis=1, mode="promise_in_bounds")
            level = jnp.where(high == i * halves + half, found, level)
        return level

    level = lax.fori_loop(0, rows, pick, jnp.zeros((slots, owners), f32), unroll=UNROLL["pick"])
    live = lax.broadcasted_iota(jnp.int32, (slots, owners), 0) < count_ref[...]
    level = jnp.where(live, level, -1.0)
    level = jnp.concatenate([level, jnp.zeros((owners - slots, owners), f32)], axis=0)
    level_ref[...] = level.T


def wide_kernel(
    taps,
    rows,
    chunk,
    gain_ref,
    near_ref,
    lines_ref,
    fields_hbm,
    inten_ref,
    fields_ref,
    table_ref,
    stack_ref,
    sems,
):
    plane = near_ref[...].astype(f32)
    stack_shifts(plane, taps, 0, stack_ref)
    table_kernel(rows, lines_ref, table_ref)
    copies = []
    for index in range(table_ref.shape[0] // chunk):
        part = pl.ds(index * chunk, chunk)
        fields_ref[part, :] = jnp.dot(
            table_ref[part, :], stack_ref[...], preferred_element_type=f32
        )
        copies.append(
            pltpu.make_async_copy(fields_ref.at[part], fields_hbm.at[part], sems.at[index])
        )
        copies[-1].start()
    total = jnp.zeros(inten_ref.shape, f32)
    for k in range(gain_ref.shape[0]):
        real = fields_ref[2 * k * rows : (2 * k + 1) * rows, :]
        imag = fields_ref[(2 * k + 1) * rows : (2 * k + 2) * rows, :]
        total = total + gain_ref[k] * (real * real + imag * imag)
    inten_ref[...] = total
    for copy in copies:
        copy.wait()


def spread(value, index, size):
    here = lax.broadcasted_iota(jnp.int32, (size, LANES), 0) == index
    return jnp.where(here, value, 0.0).astype(bf16)


def product_nt(a, b):
    return lax.dot_general(a, b, (((1,), (1,)), ((), ())), preferred_element_type=f32)


def side_by_side(ref):
    return jnp.concatenate([ref[c] for c in range(ref.shape[0])], axis=1)


def owner_kernel(
    grid_rows,
    grid_cols,
    dose_ref,
    level_ref,
    frag_ref,
    aim_ref,
    error_ref,
    slope_ref,
    level_t,
    slope_t,
    resist_ref,
    value_ref,
    place_ref,
    around_t,
):
    slots = frag_ref.shape[0]
    conds = dose_ref.shape[0]
    bins = aim_ref.shape[1] // LANES
    level_t[...] = level_ref[...].T
    dose = jnp.broadcast_to(dose_ref[...], (conds, LANES))

    def place(c, carry):
        level = jnp.broadcast_to(level_t[pl.ds(c, 1), :], (conds, LANES))
        resist = jax.nn.sigmoid(steepness * (dose * level - threshold))
        live = level >= 0.0
        resist_ref[c] = jnp.where(live, resist, 0.0)
        frag = frag_ref[pl.ds(c, 1), :]
        bin_of = jnp.broadcast_to(frag >> 7, (conds, LANES))
        value_ref[c] = jnp.concatenate(
            [jnp.where(bin_of == q, resist_ref[c], 0.0) for q in range(bins)], axis=0
        ).astype(bf16)
        place_ref[c] = spread(1.0, frag & (LANES - 1), LANES)
        return carry

    lax.fori_loop(0, slots, place, 0, unroll=UNROLL["owner"])
    total = product_nt(side_by_side(value_ref), side_by_side(place_ref))
    for q in range(bins):
        lanes = slice(q * LANES, (q + 1) * LANES)
        error_ref[:, lanes] = total[q * conds : (q + 1) * conds] - aim_ref[:, lanes]

    def answer(c, carry):
        resist = resist_ref[c]
        frag = jnp.broadcast_to(frag_ref[pl.ds(c, 1), :], (conds, LANES))
        low = frag & (LANES - 1)
        bin_of = frag >> 7
        reply = jnp.zeros((conds, LANES), f32)
        for q in range(bins):
            found = jnp.take_along_axis(
                error_ref[:, q * LANES : (q + 1) * LANES], low, axis=1, mode="promise_in_bounds"
            )
            reply = jnp.where(bin_of == q, found, reply)
        terms = reply * steepness * dose * resist * (1.0 - resist)
        slope_t[pl.ds(c, 1), :] = jnp.sum(terms, axis=0, keepdims=True)
        return carry

    lax.fori_loop(0, slots, answer, 0, unroll=UNROLL["answer"])
    slope = slope_t[:slots, :]
    lane = lax.broadcasted_iota(jnp.int32, (slots, LANES), 1)
    tile_row, tile_col = lane // grid_cols, lane % grid_cols
    for t, (down, right) in enumerate(NEIGHBOURS):
        row, col = tile_row + down, tile_col + right
        inside = (row >= 0) & (row < grid_rows) & (col >= 0) & (col < grid_cols)
        moved = pltpu.roll(slope, -(down * grid_cols + right) % LANES, axis=1)
        around_t[t * slots : (t + 1) * slots, :] = jnp.where(inside, moved, 0.0)
    rest = around_t.shape[0] - len(NEIGHBOURS) * slots
    around_t[len(NEIGHBOURS) * slots :, :] = jnp.zeros((rest, LANES), f32)
    for block in range(around_t.shape[0] // LANES):
        slope_ref[:, block, :] = around_t[block * LANES : (block + 1) * LANES, :].T


def shift_right(x, by):
    assert by & (by - 1) == 0
    return x >> (by.bit_length() - 1)


def place_sites(
    tile_rows, columns, reach, slots, reply_t, pix_refs, first_ref, second_ref, value_ref, place_ref, tall_ref, flat_ref
):
    halves = columns // LANES
    for t, (down, right) in enumerate(NEIGHBOURS):
        pix = pix_refs[right + 1][(down + 1) * slots : (down + 2) * slots, :]
        row, col = shift_right(pix, columns), pix & (columns - 1)
        row = row - (tile_rows - reach) if down < 0 else row
        height = reach if down else tile_rows
        block = pl.ds(t * slots, slots)
        if right:
            first_ref[block, :] = row
            second_ref[block, :] = col - (columns - reach) if right < 0 else col
        else:
            inside = (row >= 0) & (row < height)
            line = shift_right(col, LANES) * height + row
            first_ref[block, :] = jnp.where(inside, line, -1)
            second_ref[block, :] = col & (LANES - 1)

    def one(c, carry):
        value, where, tall, flat = [], [], [], []
        narrow, narrow_where = [], []
        for t, (down, right) in enumerate(NEIGHBOURS):
            reply = reply_t[pl.ds(t * slots + c, 1), :]
            first = first_ref[pl.ds(t * slots + c, 1), :]
            second = second_ref[pl.ds(t * slots + c, 1), :]
            height = reach if down else tile_rows
            if right:
                narrow.append(spread(reply, first, height))
                narrow_where.append(spread(1.0, second, reach))
                continue
            part = spread(reply, first, halves * height)
            (tall if down else value).append(part)
            (flat if down else where).append(spread(1.0, second, LANES))
        value_ref[c] = jnp.concatenate(value + narrow, axis=0)
        rest = jnp.zeros((place_ref.shape[1] - LANES - len(narrow_where) * reach, LANES), bf16)
        place_ref[c] = jnp.concatenate(where + narrow_where + [rest], axis=0)
        tall_ref[c] = jnp.concatenate(tall, axis=0)
        flat_ref[c] = jnp.concatenate(flat, axis=0)
        return carry

    lax.fori_loop(0, slots, one, 0, unroll=UNROLL["site"])


def finish_kernel(
    taps,
    slots,
    grid_rows,
    grid_cols,
    gain_ref,
    reply_ref,
    low_ref,
    pix_ref,
    high_ref,
    target_ref,
    inten_ref,
    fields_hbm,
    table_hbm,
    out_ref,
    fields_ref,
    table_ref,
    reply_t,
    first_ref,
    second_ref,
    value_ref,
    place_ref,
    tall_ref,
    flat_ref,
    weighted_ref,
    part_ref,
    sems,
):
    fields_copy = pltpu.make_async_copy(fields_hbm, fields_ref, sems.at[0])
    table_copy = pltpu.make_async_copy(table_hbm, table_ref, sems.at[1])
    fields_copy.start()
    table_copy.start()
    rows, columns = out_ref.shape
    height, width = inten_ref.shape
    reach = (height - rows) // 2
    halves = columns // LANES
    for block in range(reply_ref.shape[1]):
        reply_t[block * LANES : (block + 1) * LANES, :] = reply_ref[:, block, :].T
    pix_refs = (low_ref, pix_ref, high_ref)
    place_sites(
        rows, columns, reach, slots, reply_t, pix_refs, first_ref, second_ref, value_ref, place_ref, tall_ref, flat_ref
    )
    near_sum = product_nt(side_by_side(value_ref), side_by_side(place_ref))
    tall_sum = product_nt(side_by_side(tall_ref), side_by_side(flat_ref))

    def across(block, size):
        return jnp.concatenate(
            [block[half * size : (half + 1) * size] for half in range(halves)]
            + [jnp.zeros((size, width - columns), f32)],
            axis=1,
        )

    middle = near_sum[: halves * rows, :LANES]
    above = tall_sum[: halves * reach, :LANES]
    below = tall_sum[halves * reach :, LANES : 2 * LANES]
    scattered = jnp.concatenate(
        [across(above, reach), across(middle, rows), across(below, reach)], axis=0
    )
    scattered = pltpu.roll(scattered, reach, axis=1)
    start = halves * rows
    lane = lax.broadcasted_iota(jnp.int32, (height, LANES), 1)
    sides = []
    for side in range(2):
        strips = []
        for place in range(3):
            size = rows if place == 1 else reach
            strip = near_sum[start : start + size, LANES : 2 * LANES]
            shift = (side * reach - (side * 3 + place) * reach) % LANES
            strips.append(pltpu.roll(strip, shift, axis=1) if shift else strip)
            start += size
        strip = jnp.concatenate(strips, axis=0)
        here = (lane >= side * reach) & (lane < (side + 1) * reach)
        sides.append(jnp.where(here, strip, 0.0))
    gap = jnp.zeros((height, LANES), f32)
    strips = [sides[0]] + [gap] * (halves - 1) + [sides[1]]

    nominal = jax.nn.sigmoid(steepness * (inten_ref[...] - threshold))
    first = pix_ref.shape[0]
    target = jnp.concatenate([low_ref[first:, :], target_ref[...], high_ref[first:, :]], axis=1)
    target = pltpu.roll(target.astype(f32), target.shape[1] - (LANES - reach), axis=1)
    dense = (nominal - target[:, :width]) * steepness * nominal * (1.0 - nominal)
    slope = dense + scattered + jnp.concatenate(strips, axis=1)
    line = lax.broadcasted_iota(jnp.int32, (height, width), 0) - reach
    line = line + lax.axis_index("row") * rows
    column = lax.broadcasted_iota(jnp.int32, (height, width), 1) - reach
    inside = (column < columns + reach) & (line >= 0) & (line < grid_rows * rows)
    column = column + lax.axis_index("col") * columns
    inside = inside & (column >= 0) & (column < grid_cols * columns)
    slope = jnp.where(inside, slope, 0.0)

    def weigh(h, carry):
        start = pl.multiple_of(h * height, height)
        field = fields_ref[pl.ds(start, height), :]
        weighted_ref[pl.ds(start, height), :] = (gain_ref[h // 2] * field * slope).astype(bf16)
        return carry

    fields_copy.wait()
    lax.fori_loop(0, weighted_ref.shape[0] // height, weigh, 0, unroll=UNROLL["weigh"])
    table_copy.wait()
    part_ref[...] = jnp.dot(table_ref[...], weighted_ref[...], preferred_element_type=f32)

    def gather(v, total):
        start = pl.multiple_of(v * rows, rows)
        return total + pltpu.roll(part_ref[pl.ds(start, rows), :], width - v, axis=1)[:, :columns]

    total = jnp.zeros((rows, columns), f32)
    total = lax.fori_loop(0, taps, gather, total, unroll=UNROLL["gather"])
    out_ref[...] = 2.0 * total


def round_up(x, to):
    return -(-x // to) * to


def lines_of(taps, stride, length):
    count, blocks, extent = taps.shape
    padded = jnp.pad(taps, ((0, 0), (0, 0), (0, stride - extent)))
    flat = padded.reshape(count, blocks * stride)
    return jnp.pad(flat, ((0, 0), (0, length - blocks * stride))).astype(f32)


def body(mask, target, kernels, weights, doses, site_pix, send_count, recv_frag, frag_target):
    rows, columns = mask.shape
    extent = kernels.shape[-1]
    reach = extent // 2
    kernel_taps = kernels.reshape(-1, extent, extent)
    parts = kernel_taps.shape[0]
    owners, slots = site_pix.shape
    conds = doses.shape[0]
    both = ("row", "col")

    wide = 2 * reach
    pix = site_pix.T
    low, high = clipped(*ring(mask[:wide], mask[rows - wide :], "row"), "row")
    near = jnp.concatenate([low, mask, high], axis=0)
    near, pix, target = lax.optimization_barrier((near, pix, target))
    low, high = clipped(*ring(near[:, :wide], near[:, columns - wide :], "col"), "col")
    near = jnp.concatenate([low, near, high], axis=1)
    wide_columns = round_up(near.shape[1], LANES)
    near = jnp.pad(near, ((0, 0), (0, wide_columns - near.shape[1])))

    halves = columns // LANES

    def pixels_and(aim):
        lanes = [aim[:, half * LANES : (half + 1) * LANES] for half in range(halves)]
        return jnp.concatenate([pix] + lanes, axis=0)

    low, high = ring(pixels_and(target[:reach]), pixels_and(target[rows - reach :]), "row")
    pix_column = jnp.concatenate([low[:slots], pix, high[:slots]], axis=0)
    target_column = jnp.concatenate(
        [
            jnp.concatenate(
                [side[slots + half * reach :][:reach] for half in range(halves)], axis=1
            )
            if side is not None
            else target
            for side in (low, None, high)
        ],
        axis=0,
    )

    height = rows + 2 * reach
    by_column = kernel_taps.transpose(0, 2, 1)
    core_depth = round_up(extent * height, LANES)
    core_table = banded(lines_of(by_column, height, core_depth), rows)

    level = call(
        functools.partial(forward_kernel, extent, reach),
        jax.ShapeDtypeStruct((owners, LANES), f32),
        scratch=[
            pltpu.VMEM((core_depth, columns), bf16),
            pltpu.VMEM((rows * columns // LANES, LANES), f32),
        ],
        inputs=5,
        smem=(0,),
        flops=2 * parts * rows * core_depth * columns,
        moved=2 * parts * rows * core_depth,
    )(weights, near, core_table, pix, send_count)

    flipped = kernel_taps[:, ::-1, ::-1].transpose(2, 0, 1)
    back_depth = parts * height
    back_lines = lines_of(flipped, height, back_depth)
    level, pix_column, target_column, back_lines = lax.optimization_barrier(
        (level, pix_column, target_column, back_lines)
    )
    arrived = lax.all_to_all(level, both, split_axis=0, concat_axis=0, tiled=True)
    back_table = banded(back_lines, rows)
    arrived, back_table = lax.optimization_barrier((arrived, back_table))
    low, high = ring(
        jnp.concatenate([pix_column, target_column[:, :LANES]], axis=0),
        jnp.concatenate([pix_column, target_column[:, columns - LANES :]], axis=0),
        "col",
    )
    grid_rows, grid_cols = lax.axis_size("row"), lax.axis_size("col")
    blocks = round_up(len(NEIGHBOURS) * slots, LANES) // LANES
    frag_error, answers = call(
        functools.partial(owner_kernel, grid_rows, grid_cols),
        (
            jax.ShapeDtypeStruct(frag_target.shape, f32),
            jax.ShapeDtypeStruct((owners, blocks, LANES), f32),
        ),
        scratch=[
            pltpu.VMEM((LANES, LANES), f32),
            pltpu.VMEM((slots, LANES), f32),
            pltpu.VMEM((slots, conds, LANES), f32),
            pltpu.VMEM((slots, frag_target.size // LANES, LANES), bf16),
            pltpu.VMEM((slots, LANES, LANES), bf16),
            pltpu.VMEM((blocks * LANES, LANES), f32),
        ],
        inputs=4,
        flops=2 * 2 * frag_target.size * site_pix.size // 16,
        moved=8 * frag_target.size,
    )(doses[:, None], arrived, recv_frag.T, frag_target)

    tall = rows + 4 * reach
    wide_depth = round_up(extent * tall, LANES)
    wide_lines = lines_of(by_column, tall, wide_depth)
    answers, near, wide_lines = lax.optimization_barrier((answers, near, wide_lines))
    returned = lax.all_to_all(answers, both, split_axis=0, concat_axis=0, tiled=True)
    wide_fields, wide_intensity = call(
        functools.partial(wide_kernel, extent, height, parts * height // 2),
        (
            pltpu.HBM((parts * height, wide_columns), f32),
            jax.ShapeDtypeStruct((height, wide_columns), f32),
        ),
        scratch=[
            pltpu.VMEM((parts * height, wide_columns), f32),
            pltpu.VMEM((parts * height, wide_depth), bf16),
            pltpu.VMEM((wide_depth, wide_columns), bf16),
            pltpu.SemaphoreType.DMA((2,)),
        ],
        inputs=3,
        smem=(0,),
        hbm_out=(0,),
        vmem_mib=24,
        flops=2 * parts * height * wide_depth * wide_columns,
        moved=4 * parts * height * wide_columns,
    )(weights, near, wide_lines)
    returned, wide_fields, wide_intensity, low, high = lax.optimization_barrier(
        (returned, wide_fields, wide_intensity, low, high)
    )
    wide_fields = pltpu.with_memory_space_constraint(wide_fields, pltpu.HBM)
    back_table = pltpu.with_memory_space_constraint(back_table, pltpu.HBM)
    gradient = call(
        functools.partial(finish_kernel, extent, slots, grid_rows, grid_cols),
        jax.ShapeDtypeStruct((rows, columns), f32),
        scratch=[
            pltpu.VMEM(wide_fields.shape, f32),
            pltpu.VMEM(back_table.shape, bf16),
            pltpu.VMEM((blocks * LANES, LANES), f32),
            pltpu.VMEM((blocks * LANES, LANES), jnp.int32),
            pltpu.VMEM((blocks * LANES, LANES), jnp.int32),
            pltpu.VMEM((slots, halves * rows + 2 * (rows + 2 * reach), LANES), bf16),
            pltpu.VMEM((slots, 2 * LANES, LANES), bf16),
            pltpu.VMEM((slots, 2 * halves * reach, LANES), bf16),
            pltpu.VMEM((slots, 2 * LANES, LANES), bf16),
            pltpu.VMEM((back_depth, wide_columns), bf16),
            pltpu.VMEM((extent * rows, wide_columns), f32),
            pltpu.SemaphoreType.DMA((2,)),
        ],
        inputs=9,
        smem=(0,),
        hbm=(7, 8),
        vmem_mib=32,
        flops=2 * extent * rows * back_depth * wide_columns,
        moved=8 * back_depth * wide_columns,
    )(
        weights,
        returned,
        low,
        pix_column,
        high,
        target_column,
        wide_intensity,
        wide_fields,
        back_table,
    )
    return gradient, frag_error


def solution(mesh):
    return jax.shard_map(
        body,
        mesh=mesh,
        in_specs=(
            P("row", "col"),
            P("row", "col"),
            P(),
            P(),
            P(),
            P("row", "col"),
            P("row", "col"),
            P("row", "col"),
            P(None, ("row", "col")),
        ),
        out_specs=(P("row", "col"), P(None, ("row", "col"))),
        check_vma=False,
    )
```

time: 76.2 us -> 68.2 us (0.90)
  waiting for transfers between devices: 17.5 us -> 10.6 us
  Pallas kernels: 20 us -> 23.5 us
  starting transfers between devices: 31.7 us -> 28.9 us
  local copies, waits for them, and re-layouts: 5.01 us -> 3.74 us
    all_to_all x1, waiting for transfers between devices: 8.54 us -> 0.01 us  [body(): lax.all_to_all(answers, both, split_axis=0, concat_axis=0, tiled=True)]
    all_to_all x1, waiting for transfers between devices: 2.06 us -> 7.23 us  [body(): lax.all_to_all(level, both, split_axis=0, concat_axis=0, tiled=True)]
    ppermute x8, waiting for transfers between devices: 6.9 us -> 3.34 us  [ring(): return (lax.ppermute(high_end, axis, up), lax.ppermute(low_end, axis, down))]
    pallas_call x5 -> x4, Pallas kernels: 17.9 us -> 21.4 us  [the longest x1 7.73 us: body(): call(functools.partial(wide_kernel, extent, height, parts * height // 2),...]
    all_to_all x1, starting transfers between devices: 7.71 us -> 4.28 us  [body(): lax.all_to_all(answers, both, split_axis=0, concat_axis=0, tiled=True)]
    ppermute x8, starting transfers between devices: 14.7 us -> 17.4 us  [ring(): return (lax.ppermute(high_end, axis, up), lax.ppermute(low_end, axis, down))]
    all_to_all x1, starting transfers between devices: 9.31 us -> 7.16 us  [body(): lax.all_to_all(level, both, split_axis=0, concat_axis=0, tiled=True)]
    unnamed x22 -> x20, local copies, waits for them, and re-layouts: 3.88 us -> 2.67 us
  transfers between devices with their start and end apart: 10 -> 10, of which waited for: 7 -> 2; matrix products, arithmetic and copies ran while one was open for 3% -> 4% of each run, Pallas kernels for 11% -> 20%
where the time goes in v3:
time: 68.2 us; the launch traced here: 68 us
  starting transfers between devices  28.9 us (42%)
  Pallas kernels  23.5 us (34%)
  waiting for transfers between devices  10.6 us (16%)
  local copies, waits for them, and re-layouts  3.74 us (5%)
  between operations  1.15 us (2%)
    ppermute x8, starting transfers between devices, ring(): return (lax.ppermute(high_end, axis, up), lax.ppermute(low_end, axis, down))  17.4 us
    pallas_call x1, Pallas kernels, body(): call(functools.partial(wide_kernel, extent, height, parts * height // 2),...  7.73 us
    all_to_all x1, waiting for transfers between devices, body(): lax.all_to_all(level, both, split_axis=0, concat_axis=0, tiled=True)  7.23 us
    all_to_all x1, starting transfers between devices, body(): lax.all_to_all(level, both, split_axis=0, concat_axis=0, tiled=True)  7.16 us
    pallas_call x1, Pallas kernels, body(): call(functools.partial(finish_kernel, extent, slots, grid_rows, grid_cols...  6.67 us
    all_to_all x1, starting transfers between devices, body(): lax.all_to_all(answers, both, split_axis=0, concat_axis=0, tiled=True)  4.28 us
    pallas_call x1, Pallas kernels, body(): call(functools.partial(owner_kernel, grid_rows, grid_cols), (jax.ShapeDty...  3.57 us
    pallas_call x1, Pallas kernels, body(): call(functools.partial(forward_kernel, extent, reach), jax.ShapeDtypeStru...  3.45 us
  transfers between devices with their start and end apart: 10, of which 2 were waited for; matrix products, arithmetic and copies ran while one was open for 4% of the time, Pallas kernels for 20%

profile of v3, /device:TPU:1, one launch (start us, length us, event | category | flops | bytes accessed | tf_op | source)
XLA Modules:
  0.0 68.0 jit_solution(15656627177417699439)
XLA Ops:
  0.6 1.4 %collective-permute-start.1 = (bf16[32,256]{1,0:T(8,128)(2,1)}, bf16[32,256]{1,0:T(8,128)(2,1)S(1)}, u32[]{:S(2)}, u32[]{:S(2)}) collective-permute-start(bf16[32,256]{1,0:T(8,128)(2,1)} %param.9), channel_id=1, source_target_pairs={{16,0},{32,16},{48,32},{64,48},{80,64},{96,80},{112,96},{0,112},{1... | collective-permute-start | bytes 49160 | tf_op jit(solution)/shard_map/ppermute | solution.py:59
  2.1 1.2 %collective-permute-start = (bf16[32,256]{1,0:T(8,128)(2,1)}, bf16[32,256]{1,0:T(8,128)(2,1)S(1)}, u32[]{:S(2)}, u32[]{:S(2)}) collective-permute-start(bf16[32,256]{1,0:T(8,128)(2,1)} %param.9), channel_id=1, source_target_pairs={{0,16},{16,32},{32,48},{48,64},{64,80},{80,96},{96,112},{112,0},{1... | collective-permute-start | bytes 49160 | tf_op jit(solution)/shard_map/ppermute | solution.py:59
  3.3 1.0 %copy.24 = bf16[8,2,33,33]{3,1,0,2:T(2,128)(2,1)S(1)} copy(bf16[8,2,33,33]{3,1,2,0:T(2,128)(2,1)} %param.11) | data formatting | bytes 69696 | tf_op args[2]
  4.3 0.3 copy.30
  4.6 0.2 reshape.19
  4.8 0.3 copy.26
  5.1 0.1 rev.3
  5.2 0.1 reshape.20
  5.6 0.9 %shard_map.104.table_ref = bf16[512,2176]{1,0:T(8,128)(2,1)S(1)} custom-call(f32[16,2176]{1,0:T(8,128)S(1)} %pad_convert_fusion.2.lines_ref), custom_call_target="tpu_custom_call" | custom-call | bytes 2228224 | tf_op jit(solution)/shard_map/pallas_call | solution.py:86
  6.4 0.1 reshape.21.lines_ref
  6.7 6.2 %collective-permute-start.3 = (bf16[96,32]{1,0:T(8,128)(2,1)S(1)}, bf16[96,32]{1,0:T(8,128)(2,1)S(1)}, u32[]{:S(2)}, u32[]{:S(2)}) collective-permute-start(bf16[96,32]{1,0:T(8,128)(2,1)S(1)} %get-tuple-element.49), channel_id=1, source_target_pairs={{1,0},{2,1},{3,2},{4,3},{5,4},{6,5},{7,6},{8,7},{9,8},{10,9},{11,1... | collective-permute-start | bytes 18440 | tf_op jit(solution)/shard_map/ppermute | solution.py:59
  13.0 2.6 %collective-permute-start.5 = (s32[80,128]{1,0:T(8,128)S(1)}, s32[80,128]{1,0:T(8,128)S(1)}, u32[]{:S(2)}, u32[]{:S(2)}) collective-permute-start(s32[80,128]{1,0:T(8,128)S(1)} %get-tuple-element.59), channel_id=1, source_target_pairs={{16,0},{32,16},{48,32},{64,48},{80,64},{96,80},{112,96},{0,112},{1... | collective-permute-start | bytes 122888 | tf_op jit(solution)/shard_map/ppermute | solution.py:59
  15.6 3.3 %collective-permute-done.2 = bf16[96,32]{1,0:T(8,128)(2,1)S(1)} collective-permute-done((bf16[96,32]{1,0:T(8,128)(2,1)S(1)}, bf16[96,32]{1,0:T(8,128)(2,1)S(1)}, u32[]{:S(2)}, u32[]{:S(2)}) %collective-permute-start.2) | collective-permute-done | bytes 6176 | tf_op jit(solution)/shard_map/ppermute | solution.py:59
  19.1 3.4 %shard_map.105 = f32[128,128]{1,0:T(8,128)} custom-call(f32[8]{0:T(128)S(1)} %copy-done.4, bf16[96,384]{1,0:T(8,128)(2,1)S(1)} %fusion.4.mask_ref.near_ref, bf16[512,2176]{1,0:T(8,128)(2,1)S(1)} %shard_map.104.table_ref, s32[48,128]{1,0:T(8,128)S(1)} %bitcast.13, s32[1,128]{1,0:T(1,128)S(1)} %copy-done.5), custom_call_target="tpu_custom_call" | custom-call | flops 570425344 | bytes 2228224 | tf_op jit(solution)/shard_map/pallas_call | solution.py:481
  22.6 7.2 %all-to-all-start = ((f32[128,1,128]{2,1,0:T(1,128)}), f32[128,1,128]{2,1,0:T(1,128)S(1)}, u32[]{:S(2)}, u32[]{:S(2)}) async-start(f32[128,1,128]{2,1,0:T(1,128)} %bitcast.6), calls=%async_computation | async-start | bytes 131072 | tf_op jit(solution)/shard_map/all_to_all | solution.py:500
  29.8 1.2 %shard_map.106.table_hbm = bf16[1056,1024]{1,0:T(8,128)(2,1)S(1)} custom-call(f32[33,1024]{1,0:T(8,128)S(1)} %reshape.21.lines_ref), custom_call_target="tpu_custom_call" | custom-call | bytes 2162688 | tf_op jit(solution)/shard_map/pallas_call | solution.py:86
  31.0 1.4 %copy-done = bf16[1056,1024]{1,0:T(8,128)(2,1)} copy-done((bf16[1056,1024]{1,0:T(8,128)(2,1)}, bf16[1056,1024]{1,0:T(8,128)(2,1)S(1)}, u32[]{:S(2)}) %copy-start) | copy-done | bytes 2162712
  32.4 7.2 %all-to-all-done = f32[128,1,128]{2,1,0:T(1,128)S(1)} async-done(((f32[128,1,128]{2,1,0:T(1,128)}), f32[128,1,128]{2,1,0:T(1,128)S(1)}, u32[]{:S(2)}, u32[]{:S(2)}) %all-to-all-start) | async-done | bytes 65568 | tf_op jit(solution)/shard_map/all_to_all | solution.py:500
  39.6 3.6 %shard_map.107 = (f32[8,2048]{1,0:T(8,128)}, f32[128,4,128]{2,1,0:T(4,128)}) custom-call(f32[8,1]{1,0:T(8,128)S(1)} %copy.28.dose_ref, f32[128,128]{1,0:T(8,128)S(1)} %bitcast.11, s32[48,128]{1,0:T(8,128)S(1)} %bitcast.15, f32[8,2048]{1,0:T(8,128)S(1)} %copy-done.2), custom_call_target="tpu_custom_call" | custom-call | flops 25165824 | bytes 131072 | tf_op jit(solution)/shard_map/pallas_call | solution.py:510
  43.2 4.3 %all-to-all-start.1 = ((f32[128,4,128]{2,1,0:T(4,128)}), f32[128,4,128]{2,1,0:T(4,128)S(1)}, u32[]{:S(2)}, u32[]{:S(2)}) async-start(f32[128,4,128]{2,1,0:T(4,128)} %get-tuple-element.30), calls=%async_computation.1 | async-start | bytes 524288 | tf_op jit(solution)/shard_map/all_to_all | solution.py:533
  47.5 1.5 %collective-permute-start.6 = (s32[208,128]{1,0:T(8,128)S(1)}, s32[208,128]{1,0:T(8,128)S(1)}, u32[]{:S(2)}, u32[]{:S(2)}) collective-permute-start(s32[208,128]{1,0:T(8,128)S(1)} %get-tuple-element.45), channel_id=1, source_target_pairs={{0,1},{1,2},{2,3},{3,4},{4,5},{5,6},{6,7},{7,8},{8,9},{9,10},{10,1... | collective-permute-start | bytes 319496 | tf_op jit(solution)/shard_map/ppermute | solution.py:59
  49.0 4.5 %collective-permute-start.7 = (s32[208,128]{1,0:T(8,128)S(1)}, s32[208,128]{1,0:T(8,128)S(1)}, u32[]{:S(2)}, u32[]{:S(2)}) collective-permute-start(s32[208,128]{1,0:T(8,128)S(1)} %get-tuple-element.44), channel_id=1, source_target_pairs={{1,0},{2,1},{3,2},{4,3},{5,4},{6,5},{7,6},{8,7},{9,8},{10,9},{11,1... | collective-permute-start | bytes 319496 | tf_op jit(solution)/shard_map/ppermute | solution.py:59
  53.4 7.7 %shard_map.108 = (f32[1024,384]{1,0:T(8,128)}, f32[64,384]{1,0:T(8,128)S(1)}) custom-call(f32[8]{0:T(128)S(1)} %copy-done.4, bf16[96,384]{1,0:T(8,128)(2,1)S(1)} %fusion.4.mask_ref.near_ref, f32[16,3200]{1,0:T(8,128)S(1)} %pad_convert_fusion.1.lines_ref), custom_call_target="tpu_custom_call" | custom-call | flops 2516582400 | bytes 1572864 | tf_op jit(solution)/shard_map/pallas_call | solution.py:534
  61.2 6.7 %shard_map.109 = f32[32,256]{1,0:T(8,128)} custom-call(f32[8]{0:T(128)S(1)} %copy-done.4, f32[128,4,128]{2,1,0:T(4,128)S(1)} %all-to-all-done.1.reply_ref, s32[208,128]{1,0:T(8,128)S(1)} %collective-permute-done.6.low_ref, s32[144,128]{1,0:T(8,128)S(1)} %pad_add_fusion.2.pix_ref, s32[208,128]{1,0:T(8,128)S(1)} %collective-permute-done.7.high_ref, ...), custom_call_target="tpu_custom_call" | custom-call | flops 830472192 | bytes 3145728 | tf_op jit(solution)/shard_map/pallas_call | solution.py:558
  (50 shorter events, 0.6 us)
Async XLA Ops:
  0.6 4.8 %copy-start.8 = (f32[8]{0:T(128)S(1)}, f32[8]{0:T(128)}, u32[]{:S(2)}) copy-start(f32[8]{0:T(128)} %param.13) | copy-start | bytes 100
  0.6 5.9 %collective-permute-start.1 = (bf16[32,256]{1,0:T(8,128)(2,1)}, bf16[32,256]{1,0:T(8,128)(2,1)S(1)}, u32[]{:S(2)}, u32[]{:S(2)}) collective-permute-start(bf16[32,256]{1,0:T(8,128)(2,1)} %param.9), channel_id=1, source_target_pairs={{16,0},{32,16},{48,32},{64,48},{80,64},{96,80},{112,96},{0,112},{1... | collective-permute-start | bytes 49160 | tf_op jit(solution)/shard_map/ppermute | solution.py:59
  2.1 4.5 %collective-permute-start = (bf16[32,256]{1,0:T(8,128)(2,1)}, bf16[32,256]{1,0:T(8,128)(2,1)S(1)}, u32[]{:S(2)}, u32[]{:S(2)}) collective-permute-start(bf16[32,256]{1,0:T(8,128)(2,1)} %param.9), channel_id=1, source_target_pairs={{0,16},{16,32},{32,48},{48,64},{64,80},{80,96},{96,112},{112,0},{1... | collective-permute-start | bytes 49160 | tf_op jit(solution)/shard_map/ppermute | solution.py:59
  4.8 1.8 %copy-start.7 = (bf16[32,256]{1,0:T(8,128)(2,1)S(1)}, bf16[32,256]{1,0:T(8,128)(2,1)}, u32[]{:S(2)}) copy-start(bf16[32,256]{1,0:T(8,128)(2,1)} %param.9) | copy-start | bytes 49156
  5.1 7.9 %copy-start.6 = (s32[32,256]{1,0:T(8,128)S(1)}, s32[32,256]{1,0:T(8,128)}, u32[]{:S(2)}) copy-start(s32[32,256]{1,0:T(8,128)} %param.10) | copy-start | bytes 98308
  5.1 7.9 %copy-start.1 = (s32[128,48]{0,1:T(8,128)S(1)}, s32[128,48]{0,1:T(8,128)}, u32[]{:S(2)}) copy-start(s32[128,48]{0,1:T(8,128)} %param.14) | copy-start | bytes 73732
  5.4 13.7 %copy-start.4 = (f32[8]{0:T(128)S(1)}, f32[8]{0:T(128)}, u32[]{:S(2)}) copy-start(f32[8]{0:T(128)} %gain_ref.5) | copy-start | bytes 100
  5.4 13.7 %copy-start.5 = (s32[1,128]{1,0:T(1,128)S(1)}, s32[1,128]{1,0:T(1,128)}, u32[]{:S(2)}) copy-start(s32[1,128]{1,0:T(1,128)} %count_ref.1) | copy-start | bytes 1540
  6.7 8.9 %collective-permute-start.3 = (bf16[96,32]{1,0:T(8,128)(2,1)S(1)}, bf16[96,32]{1,0:T(8,128)(2,1)S(1)}, u32[]{:S(2)}, u32[]{:S(2)}) collective-permute-start(bf16[96,32]{1,0:T(8,128)(2,1)S(1)} %get-tuple-element.49), channel_id=1, source_target_pairs={{1,0},{2,1},{3,2},{4,3},{5,4},{6,5},{7,6},{8,7},{9,8},{10,9},{11,1... | collective-permute-start | bytes 18440 | tf_op jit(solution)/shard_map/ppermute | solution.py:59
  12.9 6.0 %collective-permute-start.2 = (bf16[96,32]{1,0:T(8,128)(2,1)S(1)}, bf16[96,32]{1,0:T(8,128)(2,1)S(1)}, u32[]{:S(2)}, u32[]{:S(2)}) collective-permute-start(bf16[96,32]{1,0:T(8,128)(2,1)S(1)} %get-tuple-element.48), channel_id=1, source_target_pairs={{0,1},{1,2},{2,3},{3,4},{4,5},{5,6},{6,7},{7,8},{8,9},{9,10},{10,1... | collective-permute-start | bytes 18440 | tf_op jit(solution)/shard_map/ppermute | solution.py:59
  13.0 9.6 %collective-permute-start.5 = (s32[80,128]{1,0:T(8,128)S(1)}, s32[80,128]{1,0:T(8,128)S(1)}, u32[]{:S(2)}, u32[]{:S(2)}) collective-permute-start(s32[80,128]{1,0:T(8,128)S(1)} %get-tuple-element.59), channel_id=1, source_target_pairs={{16,0},{32,16},{48,32},{64,48},{80,64},{96,80},{112,96},{0,112},{1... | collective-permute-start | bytes 122888 | tf_op jit(solution)/shard_map/ppermute | solution.py:59
  15.6 6.9 %collective-permute-start.4 = (s32[80,128]{1,0:T(8,128)S(1)}, s32[80,128]{1,0:T(8,128)S(1)}, u32[]{:S(2)}, u32[]{:S(2)}) collective-permute-start(s32[80,128]{1,0:T(8,128)S(1)} %get-tuple-element.58), channel_id=1, source_target_pairs={{0,16},{16,32},{32,48},{48,64},{64,80},{80,96},{96,112},{112,0},{1... | collective-permute-start | bytes 122888 | tf_op jit(solution)/shard_map/ppermute | solution.py:59
  19.1 20.6 %copy-start.2 = (f32[8,2048]{1,0:T(8,128)S(1)}, f32[8,2048]{1,0:T(8,128)}, u32[]{:S(2)}) copy-start(f32[8,2048]{1,0:T(8,128)} %aim_ref.1) | copy-start | bytes 196612
  19.1 20.6 %copy-start.3 = (s32[128,48]{0,1:T(8,128)S(1)}, s32[128,48]{0,1:T(8,128)}, u32[]{:S(2)}) copy-start(s32[128,48]{0,1:T(8,128)} %param.16) | copy-start | bytes 73732
  22.6 17.0 %all-to-all-start = ((f32[128,1,128]{2,1,0:T(1,128)}), f32[128,1,128]{2,1,0:T(1,128)S(1)}, u32[]{:S(2)}, u32[]{:S(2)}) async-start(f32[128,1,128]{2,1,0:T(1,128)} %bitcast.6), calls=%async_computation | async-start | bytes 131072 | tf_op jit(solution)/shard_map/all_to_all | solution.py:500
  31.0 1.4 %copy-start = (bf16[1056,1024]{1,0:T(8,128)(2,1)}, bf16[1056,1024]{1,0:T(8,128)(2,1)S(1)}, u32[]{:S(2)}) copy-start(bf16[1056,1024]{1,0:T(8,128)(2,1)S(1)} %shard_map.106.table_hbm) | copy-start | bytes 6488068
  43.2 18.0 %all-to-all-start.1 = ((f32[128,4,128]{2,1,0:T(4,128)}), f32[128,4,128]{2,1,0:T(4,128)S(1)}, u32[]{:S(2)}, u32[]{:S(2)}) async-start(f32[128,4,128]{2,1,0:T(4,128)} %get-tuple-element.30), calls=%async_computation.1 | async-start | bytes 524288 | tf_op jit(solution)/shard_map/all_to_all | solution.py:533
  47.5 13.7 %collective-permute-start.6 = (s32[208,128]{1,0:T(8,128)S(1)}, s32[208,128]{1,0:T(8,128)S(1)}, u32[]{:S(2)}, u32[]{:S(2)}) collective-permute-start(s32[208,128]{1,0:T(8,128)S(1)} %get-tuple-element.45), channel_id=1, source_target_pairs={{0,1},{1,2},{2,3},{3,4},{4,5},{5,6},{6,7},{7,8},{8,9},{9,10},{10,1... | collective-permute-start | bytes 319496 | tf_op jit(solution)/shard_map/ppermute | solution.py:59
  49.0 12.2 %collective-permute-start.7 = (s32[208,128]{1,0:T(8,128)S(1)}, s32[208,128]{1,0:T(8,128)S(1)}, u32[]{:S(2)}, u32[]{:S(2)}) collective-permute-start(s32[208,128]{1,0:T(8,128)S(1)} %get-tuple-element.44), channel_id=1, source_target_pairs={{1,0},{2,1},{3,2},{4,3},{5,4},{6,5},{7,6},{8,7},{9,8},{10,9},{11,1... | collective-permute-start | bytes 319496 | tf_op jit(solution)/shard_map/ppermute | solution.py:59

commit v4 on v3

--- a/solution.py
+++ b/solution.py
@@ -17,6 +17,7 @@
 UNROLL = {
     "table": 4,
     "stack": 33,
+    "wide": 3,
     "pick": 32,
     "owner": 4,
     "answer": 16,
@@ -71,24 +72,25 @@
     return pltpu.roll(wide, 0, axis=1, stride=1, stride_axis=0)
 
 
-def table_kernel(rows, lines_ref, out_ref):
+def fill_table(rows, first, last, lines_ref, table_ref):
     def one(index, carry):
         line = lines_ref[pl.ds(index, 1), :]
         start = pl.multiple_of(index * rows, rows)
-        out_ref[pl.ds(start, rows), :] = shear(line, rows).astype(bf16)
+        table_ref[pl.ds(start, rows), :] = shear(line, rows).astype(bf16)
         return carry
 
-    lax.fori_loop(0, lines_ref.shape[0], one, 0, unroll=UNROLL["table"])
-
-
-def banded(lines, rows, hbm=False):
-    count, width = lines.shape
-    return call(
-        functools.partial(table_kernel, rows),
-        jax.ShapeDtypeStruct((count * rows, width), bf16),
-        inputs=1,
-        moved=2 * count * rows * width,
-    )(lines)
+    lax.fori_loop(first, last, one, 0, unroll=UNROLL["table"])
+
+
+def table_kernel(rows, lines_ref, out_ref):
+    fill_table(rows, 0, lines_ref.shape[0], lines_ref, out_ref)
+
+
+def back_table_kernel(rows, lines_ref, out_hbm, out_ref, sem):
+    fill_table(rows, 0, lines_ref.shape[0], lines_ref, out_ref)
+    copy = pltpu.make_async_copy(out_ref, out_hbm, sem.at[0])
+    copy.start()
+    copy.wait()
 
 
 def stack_shifts(plane, taps, first, out_ref):
@@ -107,11 +109,24 @@
 
 
 def forward_kernel(
-    taps, reach, gain_ref, mask_ref, table_ref, pix_ref, count_ref, level_ref, stack_ref, lines_ref
+    taps,
+    reach,
+    gain_ref,
+    mask_ref,
+    table_ref,
+    pix_ref,
+    count_ref,
+    level_ref,
+    table_hbm,
+    stack_ref,
+    lines_ref,
+    sem,
 ):
     columns = stack_ref.shape[1]
     halves = columns // LANES
     rows = lines_ref.shape[0] // halves
+    store = pltpu.make_async_copy(table_ref, table_hbm, sem.at[0])
+    store.start()
     plane = mask_ref[reach : reach + rows + 2 * reach, :].astype(f32)
     stack_shifts(plane, taps, reach, stack_ref)
     fields = jnp.dot(table_ref[...], stack_ref[...], preferred_element_type=f32)
@@ -140,43 +155,75 @@
     level = jnp.where(live, level, -1.0)
     level = jnp.concatenate([level, jnp.zeros((owners - slots, owners), f32)], axis=0)
     level_ref[...] = level.T
+    store.wait()
+
+
+def stack_wide_shifts(plane, taps, columns, extra, stack_ref):
+    width = plane.shape[1]
+    height = stack_ref.shape[0] // taps // 8 * 8
+    lane = lax.broadcasted_iota(jnp.int32, (height, width - columns), 1)
+
+    def one(v, carry):
+        moved = pltpu.roll(plane, width - v, axis=1)
+        first, second = moved[:height], moved[plane.shape[0] - height :]
+        rest = pltpu.roll(second[:, columns:], extra, axis=1)
+        rest = jnp.where(lane < extra, first[:, columns:], rest)
+        start = pl.multiple_of(v * height, height)
+        stack_ref[pl.ds(start, height), :columns] = first[:, :columns].astype(bf16)
+        stack_ref[pl.ds(start, height), columns : 2 * columns] = second[:, :columns].astype(bf16)
+        stack_ref[pl.ds(start, height), 2 * columns :] = rest.astype(bf16)
+        return carry
+
+    lax.fori_loop(0, taps, one, 0, unroll=UNROLL["wide"])
+    rest = stack_ref.shape[0] - taps * height
+    stack_ref[taps * height :, :] = jnp.zeros((rest, stack_ref.shape[1]), bf16)
 
 
 def wide_kernel(
     taps,
-    rows,
-    chunk,
+    columns,
+    extra,
     gain_ref,
     near_ref,
-    lines_ref,
+    table_hbm,
     fields_hbm,
     inten_ref,
     fields_ref,
     table_ref,
     stack_ref,
-    sems,
+    in_sem,
+    out_sems,
 ):
-    plane = near_ref[...].astype(f32)
-    stack_shifts(plane, taps, 0, stack_ref)
-    table_kernel(rows, lines_ref, table_ref)
-    copies = []
-    for index in range(table_ref.shape[0] // chunk):
-        part = pl.ds(index * chunk, chunk)
-        fields_ref[part, :] = jnp.dot(
-            table_ref[part, :], stack_ref[...], preferred_element_type=f32
+    load = pltpu.make_async_copy(table_hbm, table_ref, in_sem.at[0])
+    load.start()
+    stack_wide_shifts(near_ref[...].astype(f32), taps, columns, extra, stack_ref)
+    load.wait()
+    fields = jnp.dot(table_ref[...], stack_ref[...], preferred_element_type=f32)
+    size = fields.shape[0]
+    lanes = fields.shape[1] - 2 * columns
+    rows = inten_ref.shape[0] // 2
+    stores = []
+    for half in range(2):
+        ends = fields[:, 2 * columns :]
+        if half:
+            ends = pltpu.roll(ends, lanes - extra, axis=1)
+        part = pl.ds(half * size, size)
+        fields_ref[part, :columns] = fields[:, half * columns : (half + 1) * columns]
+        fields_ref[part, columns:] = ends
+        stores.append(
+            pltpu.make_async_copy(fields_ref.at[part], fields_hbm.at[part], out_sems.at[half])
         )
-        copies.append(
-            pltpu.make_async_copy(fields_ref.at[part], fields_hbm.at[part], sems.at[index])
-        )
-        copies[-1].start()
-    total = jnp.zeros(inten_ref.shape, f32)
-    for k in range(gain_ref.shape[0]):
-        real = fields_ref[2 * k * rows : (2 * k + 1) * rows, :]
-        imag = fields_ref[(2 * k + 1) * rows : (2 * k + 2) * rows, :]
-        total = total + gain_ref[k] * (real * real + imag * imag)
-    inten_ref[...] = total
-    for copy in copies:
-        copy.wait()
+        stores[-1].start()
+    for half in range(2):
+        total = jnp.zeros((rows, inten_ref.shape[1]), f32)
+        for k in range(gain_ref.shape[0]):
+            start = half * size + 2 * k * rows
+            real = fields_ref[start : start + rows, :]
+            imag = fields_ref[start + rows : start + 2 * rows, :]
+            total = total + gain_ref[k] * (real * real + imag * imag)
+        inten_ref[half * rows : (half + 1) * rows, :] = total
+    for store in stores:
+        store.wait()
 
 
 def spread(value, index, size):
@@ -402,10 +449,16 @@
     inside = inside & (column >= 0) & (column < grid_cols * columns)
     slope = jnp.where(inside, slope, 0.0)
 
+    upper = height // 2
+    parts = weighted_ref.shape[0] // height
+
     def weigh(h, carry):
-        start = pl.multiple_of(h * height, height)
-        field = fields_ref[pl.ds(start, height), :]
-        weighted_ref[pl.ds(start, height), :] = (gain_ref[h // 2] * field * slope).astype(bf16)
+        for half in range(2):
+            lines = pl.ds(pl.multiple_of((half * parts + h) * upper, upper), upper)
+            weight = gain_ref[h // 2] * fields_ref[lines, :]
+            lines = pl.ds(pl.multiple_of(h * height + half * upper, upper), upper)
+            weighted = weight * slope[half * upper : (half + 1) * upper]
+            weighted_ref[lines, :] = weighted.astype(bf16)
         return carry
 
     fields_copy.wait()
@@ -476,29 +529,44 @@
     height = rows + 2 * reach
     by_column = kernel_taps.transpose(0, 2, 1)
     core_depth = round_up(extent * height, LANES)
-    core_table = banded(lines_of(by_column, height, core_depth), rows)
-
-    level = call(
+    core_shape = (parts * rows, core_depth)
+    core_table = call(
+        functools.partial(table_kernel, rows),
+        jax.ShapeDtypeStruct(core_shape, bf16),
+        inputs=1,
+        moved=2 * parts * rows * core_depth,
+    )(lines_of(by_column, height, core_depth))
+
+    level, stored_table = call(
         functools.partial(forward_kernel, extent, reach),
-        jax.ShapeDtypeStruct((owners, LANES), f32),
+        (jax.ShapeDtypeStruct((owners, LANES), f32), pltpu.HBM(core_shape, bf16)),
         scratch=[
             pltpu.VMEM((core_depth, columns), bf16),
             pltpu.VMEM((rows * columns // LANES, LANES), f32),
+            pltpu.SemaphoreType.DMA((1,)),
         ],
         inputs=5,
         smem=(0,),
+        hbm_out=(1,),
         flops=2 * parts * rows * core_depth * columns,
         moved=2 * parts * rows * core_depth,
     )(weights, near, core_table, pix, send_count)
 
     flipped = kernel_taps[:, ::-1, ::-1].transpose(2, 0, 1)
     back_depth = parts * height
-    back_lines = lines_of(flipped, height, back_depth)
     level, pix_column, target_column, back_lines = lax.optimization_barrier(
-        (level, pix_column, target_column, back_lines)
+        (level, pix_column, target_column, lines_of(flipped, height, back_depth))
     )
     arrived = lax.all_to_all(level, both, split_axis=0, concat_axis=0, tiled=True)
-    back_table = banded(back_lines, rows)
+    back_shape = (extent * rows, back_depth)
+    (back_table,) = call(
+        functools.partial(back_table_kernel, rows),
+        (pltpu.HBM(back_shape, bf16),),
+        scratch=[pltpu.VMEM(back_shape, bf16), pltpu.SemaphoreType.DMA((1,))],
+        inputs=1,
+        hbm_out=(0,),
+        moved=2 * extent * rows * back_depth,
+    )(back_lines)
     arrived, back_table = lax.optimization_barrier((arrived, back_table))
     low, high = ring(
         jnp.concatenate([pix_column, target_column[:, :LANES]], axis=0),
@@ -526,30 +594,29 @@
         moved=8 * frag_target.size,
     )(doses[:, None], arrived, recv_frag.T, frag_target)
 
-    tall = rows + 4 * reach
-    wide_depth = round_up(extent * tall, LANES)
-    wide_lines = lines_of(by_column, tall, wide_depth)
-    answers, near, wide_lines = lax.optimization_barrier((answers, near, wide_lines))
+    answers, near = lax.optimization_barrier((answers, near))
     returned = lax.all_to_all(answers, both, split_axis=0, concat_axis=0, tiled=True)
     wide_fields, wide_intensity = call(
-        functools.partial(wide_kernel, extent, height, parts * height // 2),
+        functools.partial(wide_kernel, extent, columns, wide),
         (
             pltpu.HBM((parts * height, wide_columns), f32),
             jax.ShapeDtypeStruct((height, wide_columns), f32),
         ),
         scratch=[
             pltpu.VMEM((parts * height, wide_columns), f32),
-            pltpu.VMEM((parts * height, wide_depth), bf16),
-            pltpu.VMEM((wide_depth, wide_columns), bf16),
+            pltpu.VMEM(core_shape, bf16),
+            pltpu.VMEM((core_depth, columns + wide_columns), bf16),
+            pltpu.SemaphoreType.DMA((1,)),
             pltpu.SemaphoreType.DMA((2,)),
         ],
         inputs=3,
         smem=(0,),
+        hbm=(2,),
         hbm_out=(0,),
         vmem_mib=24,
-        flops=2 * parts * height * wide_depth * wide_columns,
+        flops=2 * parts * rows * core_depth * (columns + wide_columns),
         moved=4 * parts * height * wide_columns,
-    )(weights, near, wide_lines)
+    )(weights, near, pltpu.with_memory_space_constraint(stored_table, pltpu.HBM))
     returned, wide_fields, wide_intensity, low, high = lax.optimization_barrier(
         (returned, wide_fields, wide_intensity, low, high)
     )

time: 68.2 us -> 66.3 us (0.972)
  local copies, waits for them, and re-layouts: 3.74 us -> 2.2 us
    unnamed x20 -> x18, local copies, waits for them, and re-layouts: 2.67 us -> 1.3 us
  transfers between devices with their start and end apart: 10 -> 10, of which waited for: 2 -> 2; matrix products, arithmetic and copies ran while one was open for 4% -> 3% of each run, Pallas kernels for 20% -> 20%
where the time goes in v4:
time: 66.3 us; the launch traced here: 66.1 us
  starting transfers between devices  29.2 us (44%)
  Pallas kernels  23.3 us (35%)
  waiting for transfers between devices  10.2 us (15%)
  local copies, waits for them, and re-layouts  2.2 us (3%)
  between operations  0.99 us (1%)
    ppermute x8, starting transfers between devices, ring(): return (lax.ppermute(high_end, axis, up), lax.ppermute(low_end, axis, down))  17.5 us
    all_to_all x1, starting transfers between devices, body(): lax.all_to_all(level, both, split_axis=0, concat_axis=0, tiled=True)  7.44 us
    all_to_all x1, waiting for transfers between devices, body(): lax.all_to_all(level, both, split_axis=0, concat_axis=0, tiled=True)  7.16 us
    pallas_call x1, Pallas kernels, body(): call(functools.partial(finish_kernel, extent, slots, grid_rows, grid_cols...  6.67 us
    pallas_call x1, Pallas kernels, body(): call(functools.partial(wide_kernel, extent, columns, wide), (pltpu.HBM((p...  6.12 us
    all_to_all x1, starting transfers between devices, body(): lax.all_to_all(answers, both, split_axis=0, concat_axis=0, tiled=True)  4.28 us
    pallas_call x1, Pallas kernels, body(): call(functools.partial(owner_kernel, grid_rows, grid_cols), (jax.ShapeDty...  3.57 us
    pallas_call x1, Pallas kernels, body(): call(functools.partial(forward_kernel, extent, reach), (jax.ShapeDtypeStr...  3.46 us
  transfers between devices with their start and end apart: 10, of which 2 were waited for; matrix products, arithmetic and copies ran while one was open for 3% of the time, Pallas kernels for 20%

profile of v4, /device:TPU:1, one launch (start us, length us, event | category | flops | bytes accessed | tf_op | source)
XLA Modules:
  0.0 66.1 jit_solution(12203325799163756664)
XLA Ops:
  0.6 1.4 %collective-permute-start.1 = (bf16[32,256]{1,0:T(8,128)(2,1)}, bf16[32,256]{1,0:T(8,128)(2,1)S(1)}, u32[]{:S(2)}, u32[]{:S(2)}) collective-permute-start(bf16[32,256]{1,0:T(8,128)(2,1)} %param.9), channel_id=1, source_target_pairs={{16,0},{32,16},{48,32},{64,48},{80,64},{96,80},{112,96},{0,112},{1... | collective-permute-start | bytes 49160 | tf_op jit(solution)/shard_map/ppermute | solution.py:60
  2.1 1.2 %collective-permute-start = (bf16[32,256]{1,0:T(8,128)(2,1)}, bf16[32,256]{1,0:T(8,128)(2,1)S(1)}, u32[]{:S(2)}, u32[]{:S(2)}) collective-permute-start(bf16[32,256]{1,0:T(8,128)(2,1)} %param.9), channel_id=1, source_target_pairs={{0,16},{16,32},{32,48},{48,64},{64,80},{80,96},{96,112},{112,0},{1... | collective-permute-start | bytes 49160 | tf_op jit(solution)/shard_map/ppermute | solution.py:60
  3.3 1.0 %copy.22 = bf16[8,2,33,33]{3,1,0,2:T(2,128)(2,1)S(1)} copy(bf16[8,2,33,33]{3,1,2,0:T(2,128)(2,1)} %param.11) | data formatting | bytes 69696 | tf_op args[2]
  4.3 0.3 copy.27
  4.6 0.2 reshape.16
  4.8 0.3 copy.24
  5.1 0.1 rev.3
  5.2 0.9 %shard_map.104.table_ref = bf16[512,2176]{1,0:T(8,128)(2,1)S(1)} custom-call(f32[16,2176]{1,0:T(8,128)S(1)} %pad_convert_fusion.1.lines_ref), custom_call_target="tpu_custom_call" | custom-call | bytes 2228224 | tf_op jit(solution)/shard_map/pallas_call | solution.py:533
  6.1 0.1 reshape.17.lines_ref
  6.4 6.2 %collective-permute-start.3 = (bf16[96,32]{1,0:T(8,128)(2,1)S(1)}, bf16[96,32]{1,0:T(8,128)(2,1)S(1)}, u32[]{:S(2)}, u32[]{:S(2)}) collective-permute-start(bf16[96,32]{1,0:T(8,128)(2,1)S(1)} %get-tuple-element.51), channel_id=1, source_target_pairs={{1,0},{2,1},{3,2},{4,3},{5,4},{6,5},{7,6},{8,7},{9,8},{10,9},{11,1... | collective-permute-start | bytes 18440 | tf_op jit(solution)/shard_map/ppermute | solution.py:60
  12.7 2.9 %collective-permute-start.5 = (s32[80,128]{1,0:T(8,128)S(1)}, s32[80,128]{1,0:T(8,128)S(1)}, u32[]{:S(2)}, u32[]{:S(2)}) collective-permute-start(s32[80,128]{1,0:T(8,128)S(1)} %get-tuple-element.61), channel_id=1, source_target_pairs={{16,0},{32,16},{48,32},{64,48},{80,64},{96,80},{112,96},{0,112},{1... | collective-permute-start | bytes 122888 | tf_op jit(solution)/shard_map/ppermute | solution.py:60
  15.6 3.0 %collective-permute-done.2 = bf16[96,32]{1,0:T(8,128)(2,1)S(1)} collective-permute-done((bf16[96,32]{1,0:T(8,128)(2,1)S(1)}, bf16[96,32]{1,0:T(8,128)(2,1)S(1)}, u32[]{:S(2)}, u32[]{:S(2)}) %collective-permute-start.2) | collective-permute-done | bytes 6176 | tf_op jit(solution)/shard_map/ppermute | solution.py:60
  18.6 0.1 fusion.4.mask_ref.near_ref
  18.8 3.5 %shard_map.105 = (f32[128,128]{1,0:T(8,128)}, bf16[512,2176]{1,0:T(8,128)(2,1)}) custom-call(f32[8]{0:T(128)S(1)} %copy-done.3, bf16[96,384]{1,0:T(8,128)(2,1)S(1)} %fusion.4.mask_ref.near_ref, bf16[512,2176]{1,0:T(8,128)(2,1)S(1)} %shard_map.104.table_ref, s32[48,128]{1,0:T(8,128)S(1)} %bitcast.13, s32[1,128]{1,0:T(1,128)S(1)} %copy-done.4), custom_call_target="tpu_custom_call" | custom-call | flops 570425344 | bytes 2228224 | tf_op jit(solution)/shard_map/pallas_call | solution.py:540
  22.4 7.4 %all-to-all-start = ((f32[128,1,128]{2,1,0:T(1,128)}), f32[128,1,128]{2,1,0:T(1,128)S(1)}, u32[]{:S(2)}, u32[]{:S(2)}) async-start(f32[128,1,128]{2,1,0:T(1,128)} %bitcast.6), calls=%async_computation | async-start | bytes 131072 | tf_op jit(solution)/shard_map/all_to_all | solution.py:560
  29.8 0.1 copy.26.dose_ref
  29.9 2.6 %shard_map.106.table_hbm = bf16[1056,1024]{1,0:T(8,128)(2,1)} custom-call(f32[33,1024]{1,0:T(8,128)S(1)} %reshape.17.lines_ref), custom_call_target="tpu_custom_call" | custom-call | bytes 2162688 | tf_op jit(solution)/shard_map/pallas_call | solution.py:562
  32.5 7.2 %all-to-all-done = f32[128,1,128]{2,1,0:T(1,128)S(1)} async-done(((f32[128,1,128]{2,1,0:T(1,128)}), f32[128,1,128]{2,1,0:T(1,128)S(1)}, u32[]{:S(2)}, u32[]{:S(2)}) %all-to-all-start) | async-done | bytes 65568 | tf_op jit(solution)/shard_map/all_to_all | solution.py:560
  39.7 3.6 %shard_map.107 = (f32[8,2048]{1,0:T(8,128)}, f32[128,4,128]{2,1,0:T(4,128)}) custom-call(f32[8,1]{1,0:T(8,128)S(1)} %copy.26.dose_ref, f32[128,128]{1,0:T(8,128)S(1)} %bitcast.11, s32[48,128]{1,0:T(8,128)S(1)} %bitcast.15, f32[8,2048]{1,0:T(8,128)S(1)} %copy-done.1), custom_call_target="tpu_custom_call" | custom-call | flops 25165824 | bytes 131072 | tf_op jit(solution)/shard_map/pallas_call | solution.py:578
  43.2 4.3 %all-to-all-start.1 = ((f32[128,4,128]{2,1,0:T(4,128)}), f32[128,4,128]{2,1,0:T(4,128)S(1)}, u32[]{:S(2)}, u32[]{:S(2)}) async-start(f32[128,4,128]{2,1,0:T(4,128)} %get-tuple-element.32), calls=%async_computation.1 | async-start | bytes 524288 | tf_op jit(solution)/shard_map/all_to_all | solution.py:598
  47.6 1.5 %collective-permute-start.6 = (s32[208,128]{1,0:T(8,128)S(1)}, s32[208,128]{1,0:T(8,128)S(1)}, u32[]{:S(2)}, u32[]{:S(2)}) collective-permute-start(s32[208,128]{1,0:T(8,128)S(1)} %get-tuple-element.47), channel_id=1, source_target_pairs={{0,1},{1,2},{2,3},{3,4},{4,5},{5,6},{6,7},{7,8},{8,9},{9,10},{10,1... | collective-permute-start | bytes 319496 | tf_op jit(solution)/shard_map/ppermute | solution.py:60
  49.0 4.3 %collective-permute-start.7 = (s32[208,128]{1,0:T(8,128)S(1)}, s32[208,128]{1,0:T(8,128)S(1)}, u32[]{:S(2)}, u32[]{:S(2)}) collective-permute-start(s32[208,128]{1,0:T(8,128)S(1)} %get-tuple-element.46), channel_id=1, source_target_pairs={{1,0},{2,1},{3,2},{4,3},{5,4},{6,5},{7,6},{8,7},{9,8},{10,9},{11,1... | collective-permute-start | bytes 319496 | tf_op jit(solution)/shard_map/ppermute | solution.py:60
  53.3 6.1 %shard_map.108 = (f32[1024,384]{1,0:T(8,128)}, f32[64,384]{1,0:T(8,128)S(1)}) custom-call(f32[8]{0:T(128)S(1)} %copy-done.3, bf16[96,384]{1,0:T(8,128)(2,1)S(1)} %fusion.4.mask_ref.near_ref, bf16[512,2176]{1,0:T(8,128)(2,1)} %get-tuple-element.34.table_hbm), custom_call_target="tpu_custom_call" | custom-call | flops 1426063360 | bytes 1572864 | tf_op jit(solution)/shard_map/pallas_call | solution.py:599
  59.5 6.7 %shard_map.109 = f32[32,256]{1,0:T(8,128)} custom-call(f32[8]{0:T(128)S(1)} %copy-done.3, f32[128,4,128]{2,1,0:T(4,128)S(1)} %all-to-all-done.1.reply_ref, s32[208,128]{1,0:T(8,128)S(1)} %collective-permute-done.6.low_ref, s32[144,128]{1,0:T(8,128)S(1)} %pad_add_fusion.2.pix_ref, s32[208,128]{1,0:T(8,128)S(1)} %collective-permute-done.7.high_ref, ...), custom_call_target="tpu_custom_call" | custom-call | flops 830472192 | bytes 3145728 | tf_op jit(solution)/shard_map/pallas_call | solution.py:625
  (45 shorter events, 0.3 us)
Async XLA Ops:
  0.6 5.6 %collective-permute-start.1 = (bf16[32,256]{1,0:T(8,128)(2,1)}, bf16[32,256]{1,0:T(8,128)(2,1)S(1)}, u32[]{:S(2)}, u32[]{:S(2)}) collective-permute-start(bf16[32,256]{1,0:T(8,128)(2,1)} %param.9), channel_id=1, source_target_pairs={{16,0},{32,16},{48,32},{64,48},{80,64},{96,80},{112,96},{0,112},{1... | collective-permute-start | bytes 49160 | tf_op jit(solution)/shard_map/ppermute | solution.py:60
  2.1 4.2 %collective-permute-start = (bf16[32,256]{1,0:T(8,128)(2,1)}, bf16[32,256]{1,0:T(8,128)(2,1)S(1)}, u32[]{:S(2)}, u32[]{:S(2)}) collective-permute-start(bf16[32,256]{1,0:T(8,128)(2,1)} %param.9), channel_id=1, source_target_pairs={{0,16},{16,32},{32,48},{48,64},{64,80},{80,96},{96,112},{112,0},{1... | collective-permute-start | bytes 49160 | tf_op jit(solution)/shard_map/ppermute | solution.py:60
  4.5 1.8 %copy-start.6 = (bf16[32,256]{1,0:T(8,128)(2,1)S(1)}, bf16[32,256]{1,0:T(8,128)(2,1)}, u32[]{:S(2)}) copy-start(bf16[32,256]{1,0:T(8,128)(2,1)} %param.9) | copy-start | bytes 49156
  4.6 8.1 %copy-start.5 = (s32[32,256]{1,0:T(8,128)S(1)}, s32[32,256]{1,0:T(8,128)}, u32[]{:S(2)}) copy-start(s32[32,256]{1,0:T(8,128)} %param.10) | copy-start | bytes 98308
  4.6 8.1 %copy-start = (s32[128,48]{0,1:T(8,128)S(1)}, s32[128,48]{0,1:T(8,128)}, u32[]{:S(2)}) copy-start(s32[128,48]{0,1:T(8,128)} %param.14) | copy-start | bytes 73732
  4.8 14.0 %copy-start.3 = (f32[8]{0:T(128)S(1)}, f32[8]{0:T(128)}, u32[]{:S(2)}) copy-start(f32[8]{0:T(128)} %gain_ref.5) | copy-start | bytes 100
  4.8 14.0 %copy-start.4 = (s32[1,128]{1,0:T(1,128)S(1)}, s32[1,128]{1,0:T(1,128)}, u32[]{:S(2)}) copy-start(s32[1,128]{1,0:T(1,128)} %count_ref.1) | copy-start | bytes 1540
  6.1 23.7 %copy-start.7 = (f32[8]{0:T(128)S(1)}, f32[8]{0:T(128)}, u32[]{:S(2)}) copy-start(f32[8]{0:T(128)} %param.13) | copy-start | bytes 100
  6.4 9.2 %collective-permute-start.3 = (bf16[96,32]{1,0:T(8,128)(2,1)S(1)}, bf16[96,32]{1,0:T(8,128)(2,1)S(1)}, u32[]{:S(2)}, u32[]{:S(2)}) collective-permute-start(bf16[96,32]{1,0:T(8,128)(2,1)S(1)} %get-tuple-element.51), channel_id=1, source_target_pairs={{1,0},{2,1},{3,2},{4,3},{5,4},{6,5},{7,6},{8,7},{9,8},{10,9},{11,1... | collective-permute-start | bytes 18440 | tf_op jit(solution)/shard_map/ppermute | solution.py:60
  12.6 6.0 %collective-permute-start.2 = (bf16[96,32]{1,0:T(8,128)(2,1)S(1)}, bf16[96,32]{1,0:T(8,128)(2,1)S(1)}, u32[]{:S(2)}, u32[]{:S(2)}) collective-permute-start(bf16[96,32]{1,0:T(8,128)(2,1)S(1)} %get-tuple-element.50), channel_id=1, source_target_pairs={{0,1},{1,2},{2,3},{3,4},{4,5},{5,6},{6,7},{7,8},{8,9},{9,10},{10,1... | collective-permute-start | bytes 18440 | tf_op jit(solution)/shard_map/ppermute | solution.py:60
  12.7 9.6 %collective-permute-start.5 = (s32[80,128]{1,0:T(8,128)S(1)}, s32[80,128]{1,0:T(8,128)S(1)}, u32[]{:S(2)}, u32[]{:S(2)}) collective-permute-start(s32[80,128]{1,0:T(8,128)S(1)} %get-tuple-element.61), channel_id=1, source_target_pairs={{16,0},{32,16},{48,32},{64,48},{80,64},{96,80},{112,96},{0,112},{1... | collective-permute-start | bytes 122888 | tf_op jit(solution)/shard_map/ppermute | solution.py:60
  15.6 6.7 %collective-permute-start.4 = (s32[80,128]{1,0:T(8,128)S(1)}, s32[80,128]{1,0:T(8,128)S(1)}, u32[]{:S(2)}, u32[]{:S(2)}) collective-permute-start(s32[80,128]{1,0:T(8,128)S(1)} %get-tuple-element.60), channel_id=1, source_target_pairs={{0,16},{16,32},{32,48},{48,64},{64,80},{80,96},{96,112},{112,0},{1... | collective-permute-start | bytes 122888 | tf_op jit(solution)/shard_map/ppermute | solution.py:60
  18.8 20.9 %copy-start.1 = (f32[8,2048]{1,0:T(8,128)S(1)}, f32[8,2048]{1,0:T(8,128)}, u32[]{:S(2)}) copy-start(f32[8,2048]{1,0:T(8,128)} %aim_ref.1) | copy-start | bytes 196612
  18.8 20.9 %copy-start.2 = (s32[128,48]{0,1:T(8,128)S(1)}, s32[128,48]{0,1:T(8,128)}, u32[]{:S(2)}) copy-start(s32[128,48]{0,1:T(8,128)} %param.16) | copy-start | bytes 73732
  22.4 17.3 %all-to-all-start = ((f32[128,1,128]{2,1,0:T(1,128)}), f32[128,1,128]{2,1,0:T(1,128)S(1)}, u32[]{:S(2)}, u32[]{:S(2)}) async-start(f32[128,1,128]{2,1,0:T(1,128)} %bitcast.6), calls=%async_computation | async-start | bytes 131072 | tf_op jit(solution)/shard_map/all_to_all | solution.py:560
  43.2 16.2 %all-to-all-start.1 = ((f32[128,4,128]{2,1,0:T(4,128)}), f32[128,4,128]{2,1,0:T(4,128)S(1)}, u32[]{:S(2)}, u32[]{:S(2)}) async-start(f32[128,4,128]{2,1,0:T(4,128)} %get-tuple-element.32), calls=%async_computation.1 | async-start | bytes 524288 | tf_op jit(solution)/shard_map/all_to_all | solution.py:598
  47.6 11.9 %collective-permute-start.6 = (s32[208,128]{1,0:T(8,128)S(1)}, s32[208,128]{1,0:T(8,128)S(1)}, u32[]{:S(2)}, u32[]{:S(2)}) collective-permute-start(s32[208,128]{1,0:T(8,128)S(1)} %get-tuple-element.47), channel_id=1, source_target_pairs={{0,1},{1,2},{2,3},{3,4},{4,5},{5,6},{6,7},{7,8},{8,9},{9,10},{10,1... | collective-permute-start | bytes 319496 | tf_op jit(solution)/shard_map/ppermute | solution.py:60
  49.0 10.4 %collective-permute-start.7 = (s32[208,128]{1,0:T(8,128)S(1)}, s32[208,128]{1,0:T(8,128)S(1)}, u32[]{:S(2)}, u32[]{:S(2)}) collective-permute-start(s32[208,128]{1,0:T(8,128)S(1)} %get-tuple-element.46), channel_id=1, source_target_pairs={{1,0},{2,1},{3,2},{4,3},{5,4},{6,5},{7,6},{8,7},{9,8},{10,9},{11,1... | collective-permute-start | bytes 319496 | tf_op jit(solution)/shard_map/ppermute | solution.py:60

commit v5 on v4

--- a/solution.py
+++ b/solution.py
@@ -19,8 +19,8 @@
     "stack": 33,
     "wide": 3,
     "pick": 32,
-    "owner": 4,
-    "answer": 16,
+    "owner": 48,
+    "answer": 24,
     "site": 4,
     "weigh": 16,
     "gather": 33,

time: 66.3 us -> 65.9 us (level)
  no operation moved by 1% of the time
where the time goes in v5:
time: 65.9 us; the launch traced here: 65.7 us
  starting transfers between devices  29.2 us (44%)
  Pallas kernels  22.8 us (35%)
  waiting for transfers between devices  10.2 us (15%)
  local copies, waits for them, and re-layouts  2.2 us (3%)
  between operations  0.99 us (2%)
    ppermute x8, starting transfers between devices, ring(): return (lax.ppermute(high_end, axis, up), lax.ppermute(low_end, axis, down))  17.5 us
    all_to_all x1, starting transfers between devices, body(): lax.all_to_all(level, both, split_axis=0, concat_axis=0, tiled=True)  7.44 us
    all_to_all x1, waiting for transfers between devices, body(): lax.all_to_all(level, both, split_axis=0, concat_axis=0, tiled=True)  7.16 us
    pallas_call x1, Pallas kernels, body(): call(functools.partial(finish_kernel, extent, slots, grid_rows, grid_cols...  6.67 us
    pallas_call x1, Pallas kernels, body(): call(functools.partial(wide_kernel, extent, columns, wide), (pltpu.HBM((p...  6.12 us
    all_to_all x1, starting transfers between devices, body(): lax.all_to_all(answers, both, split_axis=0, concat_axis=0, tiled=True)  4.28 us
    pallas_call x1, Pallas kernels, body(): call(functools.partial(forward_kernel, extent, reach), (jax.ShapeDtypeStr...  3.46 us
    pallas_call x1, Pallas kernels, body(): call(functools.partial(owner_kernel, grid_rows, grid_cols), (jax.ShapeDty...  3.12 us
  transfers between devices with their start and end apart: 10, of which 2 were waited for; matrix products, arithmetic and copies ran while one was open for 3% of the time, Pallas kernels for 20%

profile of v5, /device:TPU:1, one launch (start us, length us, event | category | flops | bytes accessed | tf_op | source)
XLA Modules:
  0.0 65.7 jit_solution(3890606349411635670)
XLA Ops:
  0.6 1.4 %collective-permute-start.1 = (bf16[32,256]{1,0:T(8,128)(2,1)}, bf16[32,256]{1,0:T(8,128)(2,1)S(1)}, u32[]{:S(2)}, u32[]{:S(2)}) collective-permute-start(bf16[32,256]{1,0:T(8,128)(2,1)} %param.9), channel_id=1, source_target_pairs={{16,0},{32,16},{48,32},{64,48},{80,64},{96,80},{112,96},{0,112},{1... | collective-permute-start | bytes 49160 | tf_op jit(solution)/shard_map/ppermute | solution.py:60
  2.1 1.2 %collective-permute-start = (bf16[32,256]{1,0:T(8,128)(2,1)}, bf16[32,256]{1,0:T(8,128)(2,1)S(1)}, u32[]{:S(2)}, u32[]{:S(2)}) collective-permute-start(bf16[32,256]{1,0:T(8,128)(2,1)} %param.9), channel_id=1, source_target_pairs={{0,16},{16,32},{32,48},{48,64},{64,80},{80,96},{96,112},{112,0},{1... | collective-permute-start | bytes 49160 | tf_op jit(solution)/shard_map/ppermute | solution.py:60
  3.3 1.0 %copy.22 = bf16[8,2,33,33]{3,1,0,2:T(2,128)(2,1)S(1)} copy(bf16[8,2,33,33]{3,1,2,0:T(2,128)(2,1)} %param.11) | data formatting | bytes 69696 | tf_op args[2]
  4.3 0.3 copy.27
  4.6 0.2 reshape.16
  4.8 0.3 copy.24
  5.1 0.1 rev.3
  5.2 0.9 %shard_map.104.table_ref = bf16[512,2176]{1,0:T(8,128)(2,1)S(1)} custom-call(f32[16,2176]{1,0:T(8,128)S(1)} %pad_convert_fusion.1.lines_ref), custom_call_target="tpu_custom_call" | custom-call | bytes 2228224 | tf_op jit(solution)/shard_map/pallas_call | solution.py:533
  6.1 0.1 reshape.17.lines_ref
  6.4 6.2 %collective-permute-start.3 = (bf16[96,32]{1,0:T(8,128)(2,1)S(1)}, bf16[96,32]{1,0:T(8,128)(2,1)S(1)}, u32[]{:S(2)}, u32[]{:S(2)}) collective-permute-start(bf16[96,32]{1,0:T(8,128)(2,1)S(1)} %get-tuple-element.51), channel_id=1, source_target_pairs={{1,0},{2,1},{3,2},{4,3},{5,4},{6,5},{7,6},{8,7},{9,8},{10,9},{11,1... | collective-permute-start | bytes 18440 | tf_op jit(solution)/shard_map/ppermute | solution.py:60
  12.7 2.9 %collective-permute-start.5 = (s32[80,128]{1,0:T(8,128)S(1)}, s32[80,128]{1,0:T(8,128)S(1)}, u32[]{:S(2)}, u32[]{:S(2)}) collective-permute-start(s32[80,128]{1,0:T(8,128)S(1)} %get-tuple-element.61), channel_id=1, source_target_pairs={{16,0},{32,16},{48,32},{64,48},{80,64},{96,80},{112,96},{0,112},{1... | collective-permute-start | bytes 122888 | tf_op jit(solution)/shard_map/ppermute | solution.py:60
  15.6 3.0 %collective-permute-done.2 = bf16[96,32]{1,0:T(8,128)(2,1)S(1)} collective-permute-done((bf16[96,32]{1,0:T(8,128)(2,1)S(1)}, bf16[96,32]{1,0:T(8,128)(2,1)S(1)}, u32[]{:S(2)}, u32[]{:S(2)}) %collective-permute-start.2) | collective-permute-done | bytes 6176 | tf_op jit(solution)/shard_map/ppermute | solution.py:60
  18.6 0.1 fusion.4.mask_ref.near_ref
  18.8 3.5 %shard_map.105 = (f32[128,128]{1,0:T(8,128)}, bf16[512,2176]{1,0:T(8,128)(2,1)}) custom-call(f32[8]{0:T(128)S(1)} %copy-done.3, bf16[96,384]{1,0:T(8,128)(2,1)S(1)} %fusion.4.mask_ref.near_ref, bf16[512,2176]{1,0:T(8,128)(2,1)S(1)} %shard_map.104.table_ref, s32[48,128]{1,0:T(8,128)S(1)} %bitcast.13, s32[1,128]{1,0:T(1,128)S(1)} %copy-done.4), custom_call_target="tpu_custom_call" | custom-call | flops 570425344 | bytes 2228224 | tf_op jit(solution)/shard_map/pallas_call | solution.py:540
  22.4 7.4 %all-to-all-start = ((f32[128,1,128]{2,1,0:T(1,128)}), f32[128,1,128]{2,1,0:T(1,128)S(1)}, u32[]{:S(2)}, u32[]{:S(2)}) async-start(f32[128,1,128]{2,1,0:T(1,128)} %bitcast.6), calls=%async_computation | async-start | bytes 131072 | tf_op jit(solution)/shard_map/all_to_all | solution.py:560
  29.8 0.1 copy.26.dose_ref
  29.9 2.6 %shard_map.106.table_hbm = bf16[1056,1024]{1,0:T(8,128)(2,1)} custom-call(f32[33,1024]{1,0:T(8,128)S(1)} %reshape.17.lines_ref), custom_call_target="tpu_custom_call" | custom-call | bytes 2162688 | tf_op jit(solution)/shard_map/pallas_call | solution.py:562
  32.5 7.2 %all-to-all-done = f32[128,1,128]{2,1,0:T(1,128)S(1)} async-done(((f32[128,1,128]{2,1,0:T(1,128)}), f32[128,1,128]{2,1,0:T(1,128)S(1)}, u32[]{:S(2)}, u32[]{:S(2)}) %all-to-all-start) | async-done | bytes 65568 | tf_op jit(solution)/shard_map/all_to_all | solution.py:560
  39.7 3.1 %shard_map.107 = (f32[8,2048]{1,0:T(8,128)}, f32[128,4,128]{2,1,0:T(4,128)}) custom-call(f32[8,1]{1,0:T(8,128)S(1)} %copy.26.dose_ref, f32[128,128]{1,0:T(8,128)S(1)} %bitcast.11, s32[48,128]{1,0:T(8,128)S(1)} %bitcast.15, f32[8,2048]{1,0:T(8,128)S(1)} %copy-done.1), custom_call_target="tpu_custom_call" | custom-call | flops 25165824 | bytes 131072 | tf_op jit(solution)/shard_map/pallas_call | solution.py:578
  42.8 4.3 %all-to-all-start.1 = ((f32[128,4,128]{2,1,0:T(4,128)}), f32[128,4,128]{2,1,0:T(4,128)S(1)}, u32[]{:S(2)}, u32[]{:S(2)}) async-start(f32[128,4,128]{2,1,0:T(4,128)} %get-tuple-element.32), calls=%async_computation.1 | async-start | bytes 524288 | tf_op jit(solution)/shard_map/all_to_all | solution.py:598
  47.1 1.5 %collective-permute-start.6 = (s32[208,128]{1,0:T(8,128)S(1)}, s32[208,128]{1,0:T(8,128)S(1)}, u32[]{:S(2)}, u32[]{:S(2)}) collective-permute-start(s32[208,128]{1,0:T(8,128)S(1)} %get-tuple-element.47), channel_id=1, source_target_pairs={{0,1},{1,2},{2,3},{3,4},{4,5},{5,6},{6,7},{7,8},{8,9},{9,10},{10,1... | collective-permute-start | bytes 319496 | tf_op jit(solution)/shard_map/ppermute | solution.py:60
  48.6 4.3 %collective-permute-start.7 = (s32[208,128]{1,0:T(8,128)S(1)}, s32[208,128]{1,0:T(8,128)S(1)}, u32[]{:S(2)}, u32[]{:S(2)}) collective-permute-start(s32[208,128]{1,0:T(8,128)S(1)} %get-tuple-element.46), channel_id=1, source_target_pairs={{1,0},{2,1},{3,2},{4,3},{5,4},{6,5},{7,6},{8,7},{9,8},{10,9},{11,1... | collective-permute-start | bytes 319496 | tf_op jit(solution)/shard_map/ppermute | solution.py:60
  52.8 6.1 %shard_map.108 = (f32[1024,384]{1,0:T(8,128)}, f32[64,384]{1,0:T(8,128)S(1)}) custom-call(f32[8]{0:T(128)S(1)} %copy-done.3, bf16[96,384]{1,0:T(8,128)(2,1)S(1)} %fusion.4.mask_ref.near_ref, bf16[512,2176]{1,0:T(8,128)(2,1)} %get-tuple-element.34.table_hbm), custom_call_target="tpu_custom_call" | custom-call | flops 1426063360 | bytes 1572864 | tf_op jit(solution)/shard_map/pallas_call | solution.py:599
  59.0 6.7 %shard_map.109 = f32[32,256]{1,0:T(8,128)} custom-call(f32[8]{0:T(128)S(1)} %copy-done.3, f32[128,4,128]{2,1,0:T(4,128)S(1)} %all-to-all-done.1.reply_ref, s32[208,128]{1,0:T(8,128)S(1)} %collective-permute-done.6.low_ref, s32[144,128]{1,0:T(8,128)S(1)} %pad_add_fusion.2.pix_ref, s32[208,128]{1,0:T(8,128)S(1)} %collective-permute-done.7.high_ref, ...), custom_call_target="tpu_custom_call" | custom-call | flops 830472192 | bytes 3145728 | tf_op jit(solution)/shard_map/pallas_call | solution.py:625
  (45 shorter events, 0.3 us)
Async XLA Ops:
  0.6 5.6 %collective-permute-start.1 = (bf16[32,256]{1,0:T(8,128)(2,1)}, bf16[32,256]{1,0:T(8,128)(2,1)S(1)}, u32[]{:S(2)}, u32[]{:S(2)}) collective-permute-start(bf16[32,256]{1,0:T(8,128)(2,1)} %param.9), channel_id=1, source_target_pairs={{16,0},{32,16},{48,32},{64,48},{80,64},{96,80},{112,96},{0,112},{1... | collective-permute-start | bytes 49160 | tf_op jit(solution)/shard_map/ppermute | solution.py:60
  2.1 4.2 %collective-permute-start = (bf16[32,256]{1,0:T(8,128)(2,1)}, bf16[32,256]{1,0:T(8,128)(2,1)S(1)}, u32[]{:S(2)}, u32[]{:S(2)}) collective-permute-start(bf16[32,256]{1,0:T(8,128)(2,1)} %param.9), channel_id=1, source_target_pairs={{0,16},{16,32},{32,48},{48,64},{64,80},{80,96},{96,112},{112,0},{1... | collective-permute-start | bytes 49160 | tf_op jit(solution)/shard_map/ppermute | solution.py:60
  4.5 1.8 %copy-start.6 = (bf16[32,256]{1,0:T(8,128)(2,1)S(1)}, bf16[32,256]{1,0:T(8,128)(2,1)}, u32[]{:S(2)}) copy-start(bf16[32,256]{1,0:T(8,128)(2,1)} %param.9) | copy-start | bytes 49156
  4.6 8.1 %copy-start.5 = (s32[32,256]{1,0:T(8,128)S(1)}, s32[32,256]{1,0:T(8,128)}, u32[]{:S(2)}) copy-start(s32[32,256]{1,0:T(8,128)} %param.10) | copy-start | bytes 98308
  4.6 8.1 %copy-start = (s32[128,48]{0,1:T(8,128)S(1)}, s32[128,48]{0,1:T(8,128)}, u32[]{:S(2)}) copy-start(s32[128,48]{0,1:T(8,128)} %param.14) | copy-start | bytes 73732
  4.8 14.0 %copy-start.3 = (f32[8]{0:T(128)S(1)}, f32[8]{0:T(128)}, u32[]{:S(2)}) copy-start(f32[8]{0:T(128)} %gain_ref.5) | copy-start | bytes 100
  4.8 14.0 %copy-start.4 = (s32[1,128]{1,0:T(1,128)S(1)}, s32[1,128]{1,0:T(1,128)}, u32[]{:S(2)}) copy-start(s32[1,128]{1,0:T(1,128)} %count_ref.1) | copy-start | bytes 1540
  6.1 23.7 %copy-start.7 = (f32[8]{0:T(128)S(1)}, f32[8]{0:T(128)}, u32[]{:S(2)}) copy-start(f32[8]{0:T(128)} %param.13) | copy-start | bytes 100
  6.4 9.2 %collective-permute-start.3 = (bf16[96,32]{1,0:T(8,128)(2,1)S(1)}, bf16[96,32]{1,0:T(8,128)(2,1)S(1)}, u32[]{:S(2)}, u32[]{:S(2)}) collective-permute-start(bf16[96,32]{1,0:T(8,128)(2,1)S(1)} %get-tuple-element.51), channel_id=1, source_target_pairs={{1,0},{2,1},{3,2},{4,3},{5,4},{6,5},{7,6},{8,7},{9,8},{10,9},{11,1... | collective-permute-start | bytes 18440 | tf_op jit(solution)/shard_map/ppermute | solution.py:60
  12.6 6.0 %collective-permute-start.2 = (bf16[96,32]{1,0:T(8,128)(2,1)S(1)}, bf16[96,32]{1,0:T(8,128)(2,1)S(1)}, u32[]{:S(2)}, u32[]{:S(2)}) collective-permute-start(bf16[96,32]{1,0:T(8,128)(2,1)S(1)} %get-tuple-element.50), channel_id=1, source_target_pairs={{0,1},{1,2},{2,3},{3,4},{4,5},{5,6},{6,7},{7,8},{8,9},{9,10},{10,1... | collective-permute-start | bytes 18440 | tf_op jit(solution)/shard_map/ppermute | solution.py:60
  12.7 9.6 %collective-permute-start.5 = (s32[80,128]{1,0:T(8,128)S(1)}, s32[80,128]{1,0:T(8,128)S(1)}, u32[]{:S(2)}, u32[]{:S(2)}) collective-permute-start(s32[80,128]{1,0:T(8,128)S(1)} %get-tuple-element.61), channel_id=1, source_target_pairs={{16,0},{32,16},{48,32},{64,48},{80,64},{96,80},{112,96},{0,112},{1... | collective-permute-start | bytes 122888 | tf_op jit(solution)/shard_map/ppermute | solution.py:60
  15.6 6.7 %collective-permute-start.4 = (s32[80,128]{1,0:T(8,128)S(1)}, s32[80,128]{1,0:T(8,128)S(1)}, u32[]{:S(2)}, u32[]{:S(2)}) collective-permute-start(s32[80,128]{1,0:T(8,128)S(1)} %get-tuple-element.60), channel_id=1, source_target_pairs={{0,16},{16,32},{32,48},{48,64},{64,80},{80,96},{96,112},{112,0},{1... | collective-permute-start | bytes 122888 | tf_op jit(solution)/shard_map/ppermute | solution.py:60
  18.8 20.9 %copy-start.1 = (f32[8,2048]{1,0:T(8,128)S(1)}, f32[8,2048]{1,0:T(8,128)}, u32[]{:S(2)}) copy-start(f32[8,2048]{1,0:T(8,128)} %aim_ref.1) | copy-start | bytes 196612
  18.8 20.9 %copy-start.2 = (s32[128,48]{0,1:T(8,128)S(1)}, s32[128,48]{0,1:T(8,128)}, u32[]{:S(2)}) copy-start(s32[128,48]{0,1:T(8,128)} %param.16) | copy-start | bytes 73732
  22.4 17.3 %all-to-all-start = ((f32[128,1,128]{2,1,0:T(1,128)}), f32[128,1,128]{2,1,0:T(1,128)S(1)}, u32[]{:S(2)}, u32[]{:S(2)}) async-start(f32[128,1,128]{2,1,0:T(1,128)} %bitcast.6), calls=%async_computation | async-start | bytes 131072 | tf_op jit(solution)/shard_map/all_to_all | solution.py:560
  42.8 16.2 %all-to-all-start.1 = ((f32[128,4,128]{2,1,0:T(4,128)}), f32[128,4,128]{2,1,0:T(4,128)S(1)}, u32[]{:S(2)}, u32[]{:S(2)}) async-start(f32[128,4,128]{2,1,0:T(4,128)} %get-tuple-element.32), calls=%async_computation.1 | async-start | bytes 524288 | tf_op jit(solution)/shard_map/all_to_all | solution.py:598
  47.1 11.9 %collective-permute-start.6 = (s32[208,128]{1,0:T(8,128)S(1)}, s32[208,128]{1,0:T(8,128)S(1)}, u32[]{:S(2)}, u32[]{:S(2)}) collective-permute-start(s32[208,128]{1,0:T(8,128)S(1)} %get-tuple-element.47), channel_id=1, source_target_pairs={{0,1},{1,2},{2,3},{3,4},{4,5},{5,6},{6,7},{7,8},{8,9},{9,10},{10,1... | collective-permute-start | bytes 319496 | tf_op jit(solution)/shard_map/ppermute | solution.py:60
  48.6 10.4 %collective-permute-start.7 = (s32[208,128]{1,0:T(8,128)S(1)}, s32[208,128]{1,0:T(8,128)S(1)}, u32[]{:S(2)}, u32[]{:S(2)}) collective-permute-start(s32[208,128]{1,0:T(8,128)S(1)} %get-tuple-element.46), channel_id=1, source_target_pairs={{1,0},{2,1},{3,2},{4,3},{5,4},{6,5},{7,6},{8,7},{9,8},{10,9},{11,1... | collective-permute-start | bytes 319496 | tf_op jit(solution)/shard_map/ppermute | solution.py:60
